TPU v7x, 128 devices: a whole 4x4x4 slice. The times are simulated.
128 devices in a mesh: seq: 8 (over y, core), tile: 16 (over z, x).
Axes of the slice: x: 4, y: 4, z: 4, core: 2. Of those that a mesh axis runs over, the one named last changes fastest.
Arguments:
- latents: bfloat16 [16384, 128], P(('seq', 'tile')), may hold values from -6 to 6
- grid_slot: int32 [16384], P(('seq', 'tile')), may hold values from 0 to 16383, as said below
- w_in: bfloat16 [432, 384], replicated, may hold values from -0.3125 to 0.3125
- b_in: float32 [384], replicated, may hold values from -3 to 3
- gain_in: float32 [384], replicated, may hold values from 0.1 to 1.9
- w_up: bfloat16 [3456, 192], replicated, may hold values from -0.109375 to 0.109375
- b_up: float32 [192], replicated, may hold values from -3 to 3
- gain_res: float32 [192], replicated, may hold values from 0.1 to 1.9
- w_res: bfloat16 [5184, 192], replicated, may hold values from -0.078125 to 0.078125
- b_res: float32 [192], replicated, may hold values from -3 to 3
Outputs:
- decoded: bfloat16 [16, 128, 49152], P(None, 'tile', 'seq')
Inputs may be any that keep to these rules, and one draw needn't show every extreme that they name: grid_slot is a permutation of 0 to 16383. Row r of the sequence lies on device r // 128 and grid row p on device p // 128 (devices in the order seq then tile). The rows of one device go to exactly 64 receiving devices, exactly 2 rows to each, so every device receives 128 rows; the receivers of device d are d + k modulo 128 for a set of offsets k common to all devices, which includes 128 / 2.
All inputs are finite; a program needn't handle non-finite values.
Results may differ from a plain program's by a relative error of at most 0.0058.
Values may be sent and summed in bfloat16 or wider, within the bound.
No kernel may reach another device: no remote copies, remote signals or barrier semaphores. Data moves between devices by JAX's collectives and lax.ppermute only.
A program may use at most 192 MiB of HBM per device.

v0:
```python
import jax
import jax.numpy as jnp
from jax import lax
from jax.sharding import PartitionSpec as P

LAT = 16
C1 = 384
C2 = 192
FS = 2
TH = 4
W = 128


def extended_2(block, sides, width):
    for axis, dim in sides:
        count = lax.axis_size(axis)
        forward = [(i, i + 1) for i in range(count - 1)]
        backward = [(target, source) for source, target in forward]
        low = lax.ppermute(
            lax.slice_in_dim(block, block.shape[dim] - width, None, axis=dim), axis, forward
        )
        high = lax.ppermute(lax.slice_in_dim(block, 0, width, axis=dim), axis, backward)
        block = jnp.concatenate([low, block, high], axis=dim)
    return block


def from_behind(x, axis, by):
    length = lax.axis_size(axis)
    pairs = [(i, i + by) for i in range(length) if 0 <= i + by < length]
    return lax.ppermute(x, axis, pairs)


def causal_taps(padded, weight, bias):
    frames = padded.shape[0] - 2
    height = padded.shape[1] - 2
    breadth = padded.shape[2] - 2
    channels = padded.shape[3]
    running = jnp.zeros((frames * height * breadth, weight.shape[1]), jnp.float32)
    for time_off in range(3):
        for row_off in range(3):
            window = jnp.concatenate(
                [
                    padded[
                        time_off : time_off + frames,
                        row_off : row_off + height,
                        col_off : col_off + breadth,
                    ]
                    for col_off in range(3)
                ],
                axis=-1,
            )
            start = (time_off * 3 + row_off) * 3 * channels
            running = running + jnp.dot(
                window.reshape(-1, 3 * channels),
                weight[start : start + 3 * channels],
                preferred_element_type=jnp.float32,
            )
    return (running + bias).reshape(frames, height, breadth, weight.shape[1])


def upsample_conv(extended, weight, bias):
    doubled = jnp.repeat(jnp.repeat(extended, 2, axis=1), 2, axis=2)[:, 1:-1, 1:-1]
    frames = doubled.shape[0]
    height = doubled.shape[1] - 2
    breadth = doubled.shape[2] - 2
    channels = doubled.shape[3]
    running = jnp.zeros((frames * height * breadth, weight.shape[1]), jnp.float32)
    for row_off in range(3):
        window = jnp.concatenate(
            [
                doubled[:, row_off : row_off + height, col_off : col_off + breadth]
                for col_off in range(3)
            ],
            axis=-1,
        )
        start = row_off * 3 * channels
        running = running + jnp.dot(
            window.reshape(-1, 3 * channels),
            weight[start : start + 3 * channels],
            preferred_element_type=jnp.float32,
        )
    return (running + bias).astype(jnp.bfloat16).reshape(frames, height, breadth, weight.shape[1])


def normed_silu(values, gain):
    scaled = values * lax.rsqrt(jnp.mean(values * values, axis=-1, keepdims=True) + 1e-06) * gain
    return jax.nn.silu(scaled).astype(jnp.bfloat16)


def local(latents, grid_slot, w_in, b_in, gain_in, w_up, b_up, gain_res, w_res, b_res):
    seq_count = lax.axis_size("seq")
    tile_count = lax.axis_size("tile")
    device_count = seq_count * tile_count
    row_count = latents.shape[0]
    row_width = latents.shape[1]
    slot_cap = 2 * row_count // device_count
    target = grid_slot // row_count
    local_row = grid_slot % row_count
    one_hot = (target[:, None] == jnp.arange(device_count, dtype=jnp.int32)[None, :]).astype(
        jnp.int32
    )
    rank_in = jnp.sum((jnp.cumsum(one_hot, axis=0) - 1) * one_hot, axis=1)
    send_slot = target * slot_cap + rank_in
    outbox = (
        jnp.zeros((device_count * slot_cap, row_width), latents.dtype).at[send_slot].set(latents)
    )
    labels = jnp.full((device_count * slot_cap,), row_count, jnp.int32).at[send_slot].set(local_row)
    inbox_rows, inbox_labels = (
        lax.all_to_all(
            outbox.reshape(device_count, slot_cap, row_width),
            ("seq", "tile"),
            split_axis=0,
            concat_axis=0,
            tiled=True,
        ),
        lax.all_to_all(
            labels.reshape(device_count, slot_cap),
            ("seq", "tile"),
            split_axis=0,
            concat_axis=0,
            tiled=True,
        ),
    )
    grid_rows = (
        jnp.zeros((row_count, row_width), jnp.bfloat16)
        .at[inbox_labels.reshape(-1)]
        .set(inbox_rows.reshape(-1, row_width), mode="drop")
    )
    grid_latent = grid_rows.reshape(FS, TH, W * LAT)
    extended = extended_2(grid_latent, (("tile", 1),), 1)
    before = from_behind(extended, "seq", 1)
    window_in = jnp.concatenate([before, extended], axis=0).reshape(FS + 2, TH + 2, W, LAT)
    window_in = jnp.pad(window_in, ((0, 0), (0, 0), (1, 1), (0, 0)))
    first_conv = causal_taps(window_in, w_in, b_in)
    first_act = normed_silu(first_conv, gain_in)
    act_ext = extended_2(first_act.reshape(FS, TH, W * C1), (("tile", 1),), 1)
    act_ext = jnp.pad(act_ext.reshape(FS, TH + 2, W, C1), ((0, 0), (0, 0), (1, 1), (0, 0)))
    section_out = upsample_conv(act_ext, w_up, b_up)
    upsampled = lax.all_to_all(
        section_out.reshape(FS, 2 * TH, 2 * W * C2), "seq", split_axis=2, concat_axis=0, tiled=True
    )
    upsampled = upsampled.reshape(FS * seq_count, 2 * TH, 2 * W // seq_count, C2)
    res_act = normed_silu(upsampled.astype(jnp.float32), gain_res)
    res_ext = extended_2(res_act, (("seq", 2), ("tile", 1)), 1)
    res_ext = jnp.pad(res_ext, ((2, 0), (0, 0), (0, 0), (0, 0)))
    res_conv = causal_taps(res_ext, w_res, b_res)
    decoded = (upsampled.astype(jnp.float32) + res_conv).astype(jnp.bfloat16)
    return decoded.reshape(decoded.shape[0], 2 * TH, -1)


def solution(mesh):
    return jax.shard_map(
        local,
        mesh=mesh,
        in_specs=(
            P(("seq", "tile"), None),
            P(("seq", "tile")),
            P(),
            P(),
            P(),
            P(),
            P(),
            P(),
            P(),
            P(),
        ),
        out_specs=P(None, "tile", "seq"),
        check_vma=False,
    )
```

profile of v0, /device:TPU:7, one launch (start us, length us, event | category | flops | bytes accessed | tf_op | source)
XLA Modules:
  0.0 614.1 jit_solution(8333284277565260925)
XLA Ops:
  2.9 10.8 %all-to-all-start = ((s32[128,1,2]{2,1,0:T(1,128)}), s32[128,1,2]{2,1,0:T(1,128)S(1)}, u32[]{:S(2)}, u32[]{:S(2)}) async-start(s32[128,1,2]{2,1,0:T(1,128)} %bitcast), calls=%async_computation | async-start | bytes 131072 | tf_op jit(solution)/shard_map/all_to_all | solution.py:116
  15.4 6.2 %all-to-all-done = s32[128,1,2]{2,1,0:T(1,128)S(1)} async-done(((s32[128,1,2]{2,1,0:T(1,128)}), s32[128,1,2]{2,1,0:T(1,128)S(1)}, u32[]{:S(2)}, u32[]{:S(2)}) %all-to-all-start) | async-done | bytes 1056 | tf_op jit(solution)/shard_map/all_to_all | solution.py:116
  21.6 6.1 all-to-all-start.1
  29.1 6.5 %all-to-all-done.1 = bf16[128,2,128]{2,1,0:T(2,128)(2,1)S(1)} async-done(((bf16[128,2,128]{2,1,0:T(2,128)(2,1)}), bf16[128,2,128]{2,1,0:T(2,128)(2,1)S(1)}, u32[]{:S(2)}, u32[]{:S(2)}) %all-to-all-start.1) | async-done | bytes 65568 | tf_op jit(solution)/shard_map/all_to_all | solution.py:109
  102.5 6.5 %collective-permute-start.3 = (bf16[2,1,49152]{2,0,1:T(2,128)(2,1)S(1)}, bf16[2,1,49152]{2,0,1:T(2,128)(2,1)S(1)}, u32[]{:S(2)}, u32[]{:S(2)}) collective-permute-start(bf16[2,1,49152]{2,0,1:T(2,128)(2,1)S(1)} %get-tuple-element.44), channel_id=1, source_target_pairs={{0,1},{1,2},{2,3},{3,4},{4,5},{5,6},{6,7},{7,8},{8,9},{9,10},{10,1... | collective-permute-start | bytes 589832 | tf_op jit(solution)/shard_map/ppermute | solution.py:19
  119.1 20.7 %fusion.57 = (bf16[2,8,256,384]{3,0,2,1:T(2,128)(2,1)S(1)}, bf16[2,8,256,384]{3,0,2,1:T(2,128)(2,1)}, bf16[2,8,256,384]{3,0,2,1:T(2,128)(2,1)}, bf16[2,8,256,384...) fusion(bf16[2,12,260,384]{3,0,2,1:T(2,128)(2,1)S(1)} %bitcast.103), kind=kLoop, calls=%fused_computation.140 | loop fusion | bytes 56623104 | tf_op jit(solution)/shard_map/slice | solution.py:71
  139.9 30.7 %pad_maximum_fusion = bf16[2,8,256,1152]{3,0,2,1:T(2,128)(2,1)} fusion(bf16[2,8,256,384]{3,0,2,1:T(2,128)(2,1)S(1)} %get-tuple-element.11, bf16[2,8,256,384]{3,0,2,1:T(2,128)(2,1)S(1)} %get-tuple-element.12, bf16[2,8,256,384]{3,0,2,1:T(2,128)(2,1)S(1)} %get-tuple-element.13), kind=kLoop, calls=%fused_computation.3 | loop fusion | flops 28311552 | bytes 18874368 | tf_op jit(solution)/shard_map/concatenate | solution.py:69
  170.6 9.1 %copy.133 = bf16[2,8,256,1152]{3,2,1,0:T(8,128)(2,1)} copy(bf16[2,8,256,1152]{3,0,2,1:T(2,128)(2,1)} %pad_maximum_fusion) | data formatting | bytes 18874368 | tf_op jit(solution)/shard_map/concatenate | solution.py:69
  179.7 13.1 %pad_maximum_fusion.1 = bf16[2,8,256,1152]{3,0,2,1:T(2,128)(2,1)} fusion(bf16[2,8,256,384]{3,0,2,1:T(2,128)(2,1)} %get-tuple-element.8, bf16[2,8,256,384]{3,0,2,1:T(2,128)(2,1)} %get-tuple-element.9, bf16[2,8,256,384]{3,0,2,1:T(2,128)(2,1)} %get-tuple-element.10), kind=kLoop, calls=%fused_computation.4 | loop fusion | flops 28311552 | bytes 18874368 | tf_op jit(solution)/shard_map/concatenate | solution.py:69
  192.7 9.1 %copy.134 = bf16[2,8,256,1152]{3,2,1,0:T(8,128)(2,1)} copy(bf16[2,8,256,1152]{3,0,2,1:T(2,128)(2,1)} %pad_maximum_fusion.1) | data formatting | bytes 18874368 | tf_op jit(solution)/shard_map/concatenate | solution.py:69
  201.8 31.2 %pad_maximum_fusion.2 = bf16[2,8,256,1152]{3,0,2,1:T(2,128)(2,1)} fusion(bf16[2,8,256,384]{3,0,2,1:T(2,128)(2,1)} %get-tuple-element.6, bf16[2,8,256,384]{3,0,2,1:T(2,128)(2,1)} %get-tuple-element.7, bf16[2,8,256,384]{3,0,2,1:T(2,128)(2,1)S(1)} %get-tuple-element.5), kind=kLoop, calls=%fused_computation.5 | loop fusion | flops 28311552 | bytes 18874368 | tf_op jit(solution)/shard_map/concatenate | solution.py:69
  233.1 9.2 %copy.135 = bf16[2,8,256,1152]{3,2,1,0:T(8,128)(2,1)} copy(bf16[2,8,256,1152]{3,0,2,1:T(2,128)(2,1)} %pad_maximum_fusion.2) | data formatting | bytes 18874368 | tf_op jit(solution)/shard_map/concatenate | solution.py:69
  242.3 7.1 %fusion.20 = f32[4096,192]{0,1:T(8,128)S(1)} fusion(bf16[4096,1152]{1,0:T(8,128)(2,1)} %bitcast.119, bf16[3456,192]{0,1:T(8,128)(2,1)S(1)} %copy-done.18), kind=kOutput, calls=%fused_computation.58 | convolution fusion | flops 1811939328 | bytes 13025280 | tf_op jit(solution)/shard_map/dot_general | solution.py:77
  249.4 7.1 %convolution_add_fusion.8 = f32[4096,192]{0,1:T(8,128)S(1)} fusion(f32[4096,192]{0,1:T(8,128)S(1)} %fusion.20, bf16[4096,1152]{1,0:T(8,128)(2,1)} %bitcast.106, bf16[3456,192]{0,1:T(8,128)(2,1)S(1)} %copy-done.18), kind=kOutput, calls=%fused_computation.35 | convolution fusion | flops 1812725760 | bytes 16171008 | tf_op jit(solution)/shard_map/dot_general | solution.py:77
  267.3 44.1 %copy.137 = bf16[2,8,49152]{1,0,2:T(2,128)(2,1)} copy(bf16[2,8,49152]{2,1,0:T(8,128)(2,1)} %reshape_reshape.3) | data formatting | bytes 3145728 | tf_op jit(solution)/shard_map/reshape;reshape | solution.py:140
  311.4 29.3 %reshape.257 = bf16[8,2,49152]{2,1,0:T(2,128)(2,1)S(1)} reshape(bf16[49152,2,8]{2,1,0:T(2,128)(2,1)} %bitcast.104) | data formatting | bytes 3145728
  340.7 24.8 %all_to_all.23 = bf16[8,2,49152]{2,1,0:T(2,128)(2,1)S(1)} all-to-all(bf16[8,2,49152]{2,1,0:T(2,128)(2,1)S(1)} %reshape.257), channel_id=1, replica_groups=mesh['seq'=8,'tile'=16] {'seq'}, dimensions={0} | all-to-all | bytes 3145728 | tf_op jit(solution)/shard_map/all_to_all | solution.py:139
  365.5 31.8 %reshape.258 = bf16[49152,2,8]{2,1,0:T(2,128)(2,1)} reshape(bf16[8,2,49152]{2,1,0:T(2,128)(2,1)S(1)} %all_to_all.23) | data formatting | bytes 3145728
  397.3 45.4 %copy.138 = bf16[2,8,49152]{2,1,0:T(8,128)(2,1)S(1)} copy(bf16[2,8,49152]{1,0,2:T(2,128)(2,1)} %bitcast.105) | data formatting | bytes 3145728 | tf_op jit(solution)/shard_map/all_to_all | solution.py:139
  461.5 6.2 %collective-permute-start.7 = (bf16[16,1,34,192]{3,2,1,0:T(8,128)(2,1)S(1)}, bf16[16,1,34,192]{3,2,1,0:T(8,128)(2,1)S(1)}, u32[]{:S(2)}, u32[]{:S(2)}) collective-permute-start(bf16[16,1,34,192]{3,2,1,0:T(8,128)(2,1)S(1)} %get-tuple-element.40), channel_id=1, source_target_pairs={{0,1},{1,2},{2,3},{3,4},{4,5},{5,6},{6,7},{7,8},{8,9},{9,10},{10,1... | collective-permute-start | bytes 626696 | tf_op jit(solution)/shard_map/ppermute | solution.py:19
  469.7 6.1 fusion.5
  493.6 14.8 %fusion.58 = (bf16[16,8,32,192]{3,2,1,0:T(8,128)(2,1)}, bf16[16,8,32,192]{3,2,1,0:T(8,128)(2,1)}, bf16[16,8,32,192]{3,2,1,0:T(8,128)(2,1)}, bf16[16,8,32,192]{3,...) fusion(bf16[18,10,34,192]{3,2,1,0:T(8,128)(2,1)S(1)} %fusion.12), kind=kLoop, calls=%fused_computation.141 | loop fusion | bytes 56623104 | tf_op jit(solution)/shard_map/slice | solution.py:43
  508.4 7.3 %pad_maximum_fusion.12 = bf16[16,8,32,576]{3,2,1,0:T(8,128)(2,1)} fusion(bf16[16,8,32,192]{3,2,1,0:T(8,128)(2,1)} %get-tuple-element.36, bf16[16,8,32,192]{3,2,1,0:T(8,128)(2,1)} %get-tuple-element.37, bf16[16,8,32,192]{3,2,1,0:T(8,128)(2,1)} %get-tuple-element.35), kind=kLoop, calls=%fused_computation.23 | loop fusion | flops 14155776 | bytes 9437184 | tf_op jit(solution)/shard_map/concatenate | solution.py:41
  515.7 6.2 %fusion.22 = f32[4096,192]{0,1:T(8,128)} fusion(bf16[4096,576]{1,0:T(8,128)(2,1)} %bitcast.114, bf16[5184,192]{0,1:T(8,128)(2,1)} %param.18), kind=kOutput, calls=%fused_computation.72 | convolution fusion | flops 905969664 | bytes 8634368 | tf_op jit(solution)/shard_map/dot_general | solution.py:53
  521.9 6.1 pad_maximum_fusion.5
  528.0 6.1 fusion.31
  542.9 6.0 convolution_add_fusion.6
  553.3 5.8 convolution_add_fusion.5
  563.6 5.8 convolution_add_fusion.4
  573.8 5.8 convolution_add_fusion.3
  584.2 5.8 convolution_add_fusion.2
  604.8 5.5 reshape.210
  (166 shorter events, 176.7 us)
Async XLA Ops:
  2.9 18.7 %all-to-all-start = ((s32[128,1,2]{2,1,0:T(1,128)}), s32[128,1,2]{2,1,0:T(1,128)S(1)}, u32[]{:S(2)}, u32[]{:S(2)}) async-start(s32[128,1,2]{2,1,0:T(1,128)} %bitcast), calls=%async_computation | async-start | bytes 131072 | tf_op jit(solution)/shard_map/all_to_all | solution.py:116
  21.6 14.1 %all-to-all-start.1 = ((bf16[128,2,128]{2,1,0:T(2,128)(2,1)}), bf16[128,2,128]{2,1,0:T(2,128)(2,1)S(1)}, u32[]{:S(2)}, u32[]{:S(2)}) async-start(bf16[128,2,128]{2,1,0:T(2,128)(2,1)} %bitcast.2), calls=%async_computation.1 | async-start | bytes 131072 | tf_op jit(solution)/shard_map/all_to_all | solution.py:109
  36.9 7.4 %collective-permute-start.1 = (bf16[2,1,2048]{2,1,0:T(2,128)(2,1)S(1)}, bf16[2,1,2048]{2,1,0:T(2,128)(2,1)S(1)}, u32[]{:S(2)}, u32[]{:S(2)}) collective-permute-start(bf16[2,1,2048]{2,1,0:T(2,128)(2,1)S(1)} %get-tuple-element.74), channel_id=1, source_target_pairs={{1,0},{2,1},{3,2},{4,3},{5,4},{6,5},{7,6},{8,7},{9,8},{10,9},{11,1... | collective-permute-start | bytes 24584 | tf_op jit(solution)/shard_map/ppermute | solution.py:22
  39.3 5.9 collective-permute-start
  45.2 5.7 collective-permute-start.2
  56.2 6.2 %copy-start.15 = (bf16[2,4,128,16]{3,2,0,1:T(8,128)(2,1)S(1)}, bf16[2,4,128,16]{3,2,0,1:T(8,128)(2,1)}, u32[]{:S(2)}) copy-start(bf16[2,4,128,16]{3,2,0,1:T(8,128)(2,1)} %get-tuple-element.54) | copy-start | bytes 98308
  56.2 6.2 %copy-start.16 = (bf16[2,4,128,16]{3,2,0,1:T(8,128)(2,1)S(1)}, bf16[2,4,128,16]{3,2,0,1:T(8,128)(2,1)}, u32[]{:S(2)}) copy-start(bf16[2,4,128,16]{3,2,0,1:T(8,128)(2,1)} %get-tuple-element.68) | copy-start | bytes 98308
  62.3 9.5 %copy-start.14 = (bf16[2,4,128,16]{3,2,0,1:T(8,128)(2,1)S(1)}, bf16[2,4,128,16]{3,2,0,1:T(8,128)(2,1)}, u32[]{:S(2)}) copy-start(bf16[2,4,128,16]{3,2,0,1:T(8,128)(2,1)} %get-tuple-element.50) | copy-start | bytes 98308
  71.8 9.6 %copy-start.12 = (bf16[2,4,128,16]{3,2,0,1:T(8,128)(2,1)S(1)}, bf16[2,4,128,16]{3,2,0,1:T(8,128)(2,1)}, u32[]{:S(2)}) copy-start(bf16[2,4,128,16]{3,2,0,1:T(8,128)(2,1)} %get-tuple-element.71) | copy-start | bytes 98308
  71.8 9.6 %copy-start.13 = (bf16[2,4,128,16]{3,2,0,1:T(8,128)(2,1)S(1)}, bf16[2,4,128,16]{3,2,0,1:T(8,128)(2,1)}, u32[]{:S(2)}) copy-start(bf16[2,4,128,16]{3,2,0,1:T(8,128)(2,1)} %get-tuple-element.72) | copy-start | bytes 98308
  81.4 6.0 copy-start.21
  95.8 13.2 %copy-start.19 = (f32[384]{0:T(512)S(1)}, f32[384]{0:T(512)}, u32[]{:S(2)}) copy-start(f32[384]{0:T(512)} %param.14) | copy-start | bytes 4612
  100.6 10.5 %collective-permute-start.4 = (bf16[2,1,49152]{2,0,1:T(2,128)(2,1)S(1)}, bf16[2,1,49152]{2,0,1:T(2,128)(2,1)S(1)}, u32[]{:S(2)}, u32[]{:S(2)}) collective-permute-start(bf16[2,1,49152]{2,0,1:T(2,128)(2,1)S(1)} %get-tuple-element.45), channel_id=1, source_target_pairs={{1,0},{2,1},{3,2},{4,3},{5,4},{6,5},{7,6},{8,7},{9,8},{10,9},{11,1... | collective-permute-start | bytes 589832 | tf_op jit(solution)/shard_map/ppermute | solution.py:22
  102.5 10.3 %collective-permute-start.3 = (bf16[2,1,49152]{2,0,1:T(2,128)(2,1)S(1)}, bf16[2,1,49152]{2,0,1:T(2,128)(2,1)S(1)}, u32[]{:S(2)}, u32[]{:S(2)}) collective-permute-start(bf16[2,1,49152]{2,0,1:T(2,128)(2,1)S(1)} %get-tuple-element.44), channel_id=1, source_target_pairs={{0,1},{1,2},{2,3},{3,4},{4,5},{5,6},{6,7},{7,8},{8,9},{9,10},{10,1... | collective-permute-start | bytes 589832 | tf_op jit(solution)/shard_map/ppermute | solution.py:19
  233.0 9.2 %copy-start.18 = (bf16[3456,192]{0,1:T(8,128)(2,1)S(1)}, bf16[3456,192]{0,1:T(8,128)(2,1)}, u32[]{:S(2)}) copy-start(bf16[3456,192]{0,1:T(8,128)(2,1)} %param.15) | copy-start | bytes 3981316
  242.3 14.2 %slice-start = ((s8[9437184]{0:T(1024)(128)(4,1)}), s8[4194304]{0:T(1024)(128)(4,1)S(1)}, s32[]{:S(2)}) async-start(s8[9437184]{0:T(1024)(128)(4,1)} %bitcast.120), calls=%async_computation.3 | async-start | bytes 8388608
  242.3 14.2 %slice-start.1 = ((s8[9437184]{0:T(1024)(128)(4,1)}), s8[4194304]{0:T(1024)(128)(4,1)S(1)}, s32[]{:S(2)}) async-start(s8[9437184]{0:T(1024)(128)(4,1)} %bitcast.120), calls=%async_computation.4 | async-start | bytes 8388608
  249.4 7.1 %slice-start.2 = ((s8[9437184]{0:T(1024)(128)(4,1)}), s8[1048576]{0:T(1024)(128)(4,1)S(1)}, s32[]{:S(2)}) async-start(s8[9437184]{0:T(1024)(128)(4,1)} %bitcast.120), calls=%async_computation.5 | async-start | bytes 2097152
  249.4 7.1 %copy-start.23 = (f32[192]{0:T(256)S(1)}, f32[192]{0:T(256)}, u32[]{:S(2)}) copy-start(f32[192]{0:T(256)} %param.16) | copy-start | bytes 2308
  453.7 6.3 %collective-permute-start.6 = (bf16[16,8,1,192]{3,2,1,0:T(2,128)(2,1)S(1)}, bf16[16,8,1,192]{3,2,1,0:T(2,128)(2,1)S(1)}, u32[]{:S(2)}, u32[]{:S(2)}) collective-permute-start(bf16[16,8,1,192]{3,2,1,0:T(2,128)(2,1)S(1)} %get-tuple-element.43), channel_id=1, source_target_pairs={{16,0},{32,16},{48,32},{64,48},{80,64},{96,80},{112,96},{17,1},{33... | collective-permute-start | bytes 147464 | tf_op jit(solution)/shard_map/ppermute | solution.py:22
  456.6 4.5 collective-permute-start.5
  461.5 14.3 %collective-permute-start.7 = (bf16[16,1,34,192]{3,2,1,0:T(8,128)(2,1)S(1)}, bf16[16,1,34,192]{3,2,1,0:T(8,128)(2,1)S(1)}, u32[]{:S(2)}, u32[]{:S(2)}) collective-permute-start(bf16[16,1,34,192]{3,2,1,0:T(8,128)(2,1)S(1)} %get-tuple-element.40), channel_id=1, source_target_pairs={{0,1},{1,2},{2,3},{3,4},{4,5},{5,6},{6,7},{7,8},{8,9},{9,10},{10,1... | collective-permute-start | bytes 626696 | tf_op jit(solution)/shard_map/ppermute | solution.py:19
  467.7 13.0 %collective-permute-start.8 = (bf16[16,1,34,192]{3,2,1,0:T(8,128)(2,1)S(1)}, bf16[16,1,34,192]{3,2,1,0:T(8,128)(2,1)S(1)}, u32[]{:S(2)}, u32[]{:S(2)}) collective-permute-start(bf16[16,1,34,192]{3,2,1,0:T(8,128)(2,1)S(1)} %get-tuple-element.41), channel_id=1, source_target_pairs={{1,0},{2,1},{3,2},{4,3},{5,4},{6,5},{7,6},{8,7},{9,8},{10,9},{11,1... | collective-permute-start | bytes 626696 | tf_op jit(solution)/shard_map/ppermute | solution.py:22
  515.7 6.2 %copy-start.9 = (bf16[16,8,32,192]{3,2,1,0:T(8,128)(2,1)S(1)}, bf16[16,8,32,192]{3,2,1,0:T(8,128)(2,1)}, u32[]{:S(2)}) copy-start(bf16[16,8,32,192]{3,2,1,0:T(8,128)(2,1)} %get-tuple-element.29) | copy-start | bytes 4718596
  534.2 4.3 copy-start.8
  542.9 6.0 copy-start.7
  553.3 5.8 copy-start.6
  563.6 5.8 copy-start.5
  573.8 5.8 copy-start.4
  584.2 5.8 copy-start.10
  594.4 4.1 copy-start.3
  604.8 5.5 copy-start.2
  (6 other events, 19.2 us)
where the time goes:
time: 624 us; the launch traced here: 614 us
  local copies, waits for them, and re-layouts  272 us (44%)
  other arithmetic  153 us (25%)
  matrix products  88.2 us (14%)
  starting transfers between devices  50.7 us (8%)
  blocking collectives  24.8 us (4%)
  waiting for transfers between devices  23.7 us (4%)
    concatenate x3, other arithmetic, upsample_conv(): jnp.concatenate([doubled[:, row_off:row_off + height, col_off:col_off + b...  75 us
    dot_general x18, matrix products, causal_taps(): jnp.dot(window.reshape(-1, 3 * channels), weight[start:start + 3 * channe...  69.6 us
    unnamed x60, local copies, waits for them, and re-layouts  64 us
    concatenate x14, other arithmetic, causal_taps(): jnp.concatenate([padded[time_off:time_off + frames, row_off:row_off + hei...  54.5 us
    another operation x2, local copies, waits for them, and re-layouts, local(): section_out.reshape(FS, 2 * TH, 2 * W * C2)  47.3 us
    all_to_all x1, local copies, waits for them, and re-layouts, local(): lax.all_to_all(section_out.reshape(FS, 2 * TH, 2 * W * C2), 'seq', split_...  45.4 us
    concatenate x3, local copies, waits for them, and re-layouts, upsample_conv(): jnp.concatenate([doubled[:, row_off:row_off + height, col_off:col_off + b...  27.4 us
    slice x6, local copies, waits for them, and re-layouts, causal_taps(): padded[time_off:time_off + frames, row_off:row_off + height, col_off:col_...  27.3 us
  transfers between devices with their start and end apart: 11, of which 8 were waited for; matrix products, arithmetic and copies ran while one was open for 2% of the time, Pallas kernels for 0%

commit v1 on v0

v1 whole, which is shorter than its diff:
```python
import jax
import jax.numpy as jnp
from jax import lax
from jax.experimental import pallas as pl
from jax.experimental.pallas import tpu as pltpu
from jax.sharding import PartitionSpec as P

F32 = jnp.float32
BF16 = jnp.bfloat16
I32 = jnp.int32


def iota(shape, dim):
    return lax.broadcasted_iota(I32, shape, dim)


def ones_where(cond):
    return jnp.where(cond, 1.0, 0.0).astype(BF16)


def outbox_kernel(slot_ref, lat_ref, out_ref):
    n = 128
    row = jnp.broadcast_to(slot_ref[...], (n, n))
    col = jnp.transpose(row)
    i, j = iota((n, n), 0), iota((n, n), 1)
    same = (row >> 7) == (col >> 7)
    rank_row = jnp.sum(jnp.where(same & (i < j), 1, 0), axis=0, keepdims=True)
    rank_col = jnp.sum(jnp.where(same & (j < i), 1, 0), axis=1, keepdims=True)

    def keys(slot, rank):
        target = slot >> 7
        band = target & 15
        frame, high, group = (slot >> 6) & 1, (slot >> 4) & 3, slot & 15
        upper = high < 2
        halo_target = jnp.where(upper, target - 1, target + 1)
        inside = (upper & (band > 0)) | ((high >= 2) & (band < 15))
        halo_target = jnp.where(inside, halo_target, -1000)
        halo_slot = jnp.where(upper, 4, 2) + rank
        own_label = (frame * 8 + high + 2) * 16 + group + 1
        halo_label = (frame * 8 + jnp.where(upper, high + 6, high - 2)) * 16 + group + 1
        return target, halo_target, halo_slot, own_label, halo_label

    target, halo_target, halo_slot, _, _ = keys(slot_ref[...], rank_row)
    _, _, halo_slot_col, own_label, halo_label = keys(col, rank_col)
    own_table = jnp.where(j == rank_col, own_label, 0).astype(F32).astype(BF16)
    halo_table = jnp.where(j == halo_slot_col, halo_label, 0).astype(F32).astype(BF16)

    q = iota((8 * n, n), 0)
    pick = ones_where((q == target * 8 + rank_row) | (q == halo_target * 8 + halo_slot))
    pick_own = ones_where(q == target * 8 + 6)
    pick_halo = ones_where(q == halo_target * 8 + 6)
    out = jnp.dot(pick, lat_ref[...], preferred_element_type=F32)
    out += jnp.dot(pick_own, own_table, preferred_element_type=F32)
    out += jnp.dot(pick_halo, halo_table, preferred_element_type=F32)
    out_ref[...] = out.astype(BF16)


def route_kernel(inbox_ref, out_ref):
    rows = inbox_ref.shape[0]
    inbox = inbox_ref[...]
    boxes = inbox.astype(F32).reshape(rows // 8, 8, 128)
    labels = jnp.broadcast_to(boxes[:, 6:7, :], boxes.shape)
    slot, lane = iota(boxes.shape, 1), iota(boxes.shape, 2)
    label = jnp.sum(jnp.where((slot == lane) & (slot < 6), labels, 0.0), axis=2, keepdims=True)
    label = label.reshape(rows, 1).astype(I32)
    k = iota((1, 512), 1)
    group = 2 * (k >> 6) - 1 + ((k >> 1) & 3)
    wanted = ((k & 1) * 8 + ((k >> 3) & 7)) * 16 + group + 1
    wanted = jnp.where((group >= 0) & (group < 16), wanted, -1)
    pick = ones_where(label == wanted)
    out = lax.dot_general(pick, inbox, (((0,), (0,)), ((), ())), preferred_element_type=F32)
    out_ref[...] = out.astype(BF16)


def silu(v):
    half = 0.5 * v
    return half * jnp.tanh(half) + half


def decode_kernel(
    recv_ref, w1_ref, b1_ref, g1_ref, wc_ref, bc_ref, g2_ref, w0_ref, wp_ref, b3_ref,
    out_ref, grid_ref, x_ref, a_ref, u_ref, acc_ref, r_ref, fin_ref,
):
    s = lax.axis_index("seq")
    t = lax.axis_index("tile")
    lane = iota((1, 128), 1)

    i, k = iota((1536, 512), 0), iota((1536, 512), 1)
    key_i = ((i >> 4) & 31) * 32 + (i & 15) - 2 + (i >> 9)
    key_k = ((k >> 1) & 31) * 32 + 2 * (k >> 6) + (k & 1)
    grid_ref[...] = jnp.dot(
        ones_where(key_i == key_k), recv_ref[...], preferred_element_type=F32
    ).reshape(3, 8, 4, 16, 128)

    def windows(y, carry):
        tiles = [[grid_ref[d, y, c] for c in range(4)] for d in range(3)]
        for ix in range(18):
            c, o = divmod((ix + 6) * 16, 128)

            def window(d, to):
                tile = tiles[d][c]
                if o + 48 > 128:
                    tile = jnp.where(lane >= o, tile, tiles[d][c + 1])
                shift = (to - o) % 128
                return pltpu.roll(tile, shift, 1) if shift else tile

            x_ref[y, ix, :, 0:128] = jnp.where(lane < 64, window(0, 0), window(1, 64)).astype(BF16)
            x_ref[y, ix, :, 128:256] = window(2, 0).astype(BF16)
        return carry

    lax.fori_loop(0, 8, windows, 0)

    def first(iy, carry):
        lhs = jnp.concatenate([x_ref[iy + d].reshape(288, 256) for d in range(3)], axis=1)
        v = jnp.dot(lhs, w1_ref[...], preferred_element_type=F32) + b1_ref[...]
        scale = lax.rsqrt(jnp.mean(v * v, axis=1, keepdims=True) + 1e-06)
        a_ref[iy] = silu(v * scale * g1_ref[...]).astype(BF16).reshape(18, 16, 384)
        return carry

    lax.fori_loop(0, 6, first, 0)

    @pl.when(t == 0)
    def _():
        a_ref[0] = jnp.zeros((18, 16, 384), BF16)

    @pl.when(t == lax.axis_size("tile") - 1)
    def _():
        a_ref[5] = jnp.zeros((18, 16, 384), BF16)

    @pl.when(s == 0)
    def _():
        a_ref[:, 0] = jnp.zeros((6, 16, 384), BF16)

    @pl.when(s == lax.axis_size("seq") - 1)
    def _():
        a_ref[:, 17] = jnp.zeros((6, 16, 384), BF16)

    def corners(ci, carry):
        lhs = jnp.concatenate(
            [a_ref[ci + d, pl.ds(e, 17)].reshape(272, 384) for d in range(2) for e in range(2)],
            axis=1,
        )
        acc_ref[...] = jnp.dot(lhs, wc_ref[...], preferred_element_type=F32)
        for d in range(2):
            u = (acc_ref[:, 384 * d : 384 * d + 384] + bc_ref[...]).astype(BF16)
            u_ref[2 * ci + d] = u.reshape(17, 16, 384)
            u = u.astype(F32)
            sq = u * u
            mid = sq[:, 128:256]
            low = jnp.sum(sq[:, 0:128] + jnp.where(lane < 64, mid, 0.0), axis=1, keepdims=True)
            top = jnp.sum(sq[:, 256:384] + jnp.where(lane < 64, 0.0, mid), axis=1, keepdims=True)
            low = lax.rsqrt(low * (1 / 192) + 1e-06)
            top = lax.rsqrt(top * (1 / 192) + 1e-06)
            low = jnp.broadcast_to(low, (272, 128))
            top = jnp.broadcast_to(top, (272, 128))
            scale = jnp.concatenate([low, jnp.where(lane < 64, low, top), top], axis=1)
            r = silu(u * scale * g2_ref[...]).reshape(17, 16, 384)
            frame = iota((1, 16, 384), 1)
            r_ref[2, 2 * ci + d] = r.astype(BF16)
            for shift in (1, 2):
                moved = jnp.where(frame >= shift, pltpu.roll(r, shift, 1), 0.0)
                r_ref[2 - shift, 2 * ci + d] = moved.astype(BF16)
        return carry

    lax.fori_loop(0, 5, corners, 0)

    @pl.when(t == 0)
    def _():
        for d in range(3):
            r_ref[d, 0] = jnp.zeros((17, 16, 384), BF16)

    @pl.when(t == lax.axis_size("tile") - 1)
    def _():
        for d in range(3):
            r_ref[d, 9] = jnp.zeros((17, 16, 384), BF16)

    wide = iota((1, 1, 384), 2)

    @pl.when(s == 0)
    def _():
        for d in range(3):
            r_ref[d, :, 0] = jnp.where(wide < 192, r_ref[d, :, 0].astype(F32), 0.0).astype(BF16)

    @pl.when(s == lax.axis_size("seq") - 1)
    def _():
        for d in range(3):
            r_ref[d, :, 16] = jnp.where(wide < 192, 0.0, r_ref[d, :, 16].astype(F32)).astype(BF16)

    def residual(y, carry):
        even, odd = [], []
        for d in range(3):
            for e in range(3):
                even.append(r_ref[d, y + e, pl.ds(0, 16), :, :].reshape(256, 384))
                even.append(r_ref[d, y + e, pl.ds(1, 16), :, 128:384].reshape(256, 256))
                odd.append(r_ref[d, y + e, pl.ds(0, 16), :, 0:256].reshape(256, 256))
                odd.append(r_ref[d, y + e, pl.ds(1, 16), :, :].reshape(256, 384))
        p = jnp.dot(jnp.concatenate(even, axis=1), w0_ref[...], preferred_element_type=F32)
        q = jnp.dot(jnp.concatenate(odd, axis=1), wp_ref[...], preferred_element_type=F32)
        left = u_ref[y + 1, pl.ds(0, 16)].reshape(256, 384).astype(F32)
        right = u_ref[y + 1, pl.ds(1, 16)].reshape(256, 384).astype(F32)
        b3 = b3_ref[...]
        at = pl.ds(pl.multiple_of(y * 256, 256), 256)
        fin_ref[0, at, :] = p[:, 0:128] + b3[:, 0:128] + left[:, 0:128]
        fin_ref[1, at, :] = (
            p[:, 128:256] + q[:, 0:128] + b3[:, 128:256]
            + jnp.where(lane < 64, left[:, 128:256], right[:, 128:256])
        )
        fin_ref[2, at, :] = q[:, 128:256] + b3[:, 256:384] + right[:, 256:384]
        return carry

    lax.fori_loop(0, 8, residual, 0)

    def finish(f, carry):
        for m in range(16):
            for c in range(3):
                rows = fin_ref[c, pl.ds(m * 16 + f, 8, stride=256), :]
                out_ref[f, :, 384 * m + 128 * c : 384 * m + 128 * c + 128] = rows.astype(BF16)
        return carry

    lax.fori_loop(0, 16, finish, 0)


def first_weights(w_in):
    w = w_in.reshape(3, 3, 48, 384).transpose(1, 0, 2, 3)
    return jnp.pad(w, ((0, 0), (0, 1), (0, 16), (0, 0))).reshape(768, 384)


def corner_weights(w_up):
    w = w_up.reshape(3, 3, 384, 192).astype(F32)
    rows = [[w[0] + w[1], w[2]], [w[0], w[1] + w[2]]]

    def columns(v):
        return [[v[0] + v[1], v[2]], [v[0], v[1] + v[2]]]

    blocks = []
    for r in range(2):
        for c in range(2):
            across = [columns(rows[dy][r])[dx][c] for dy in range(2) for dx in (1, 0)]
            blocks.append(jnp.concatenate(across, axis=1))
    return jnp.concatenate(blocks, axis=0).astype(BF16)


def residual_weights(w_res):
    w = w_res.reshape(9, 3, 192, 192)
    zero = jnp.zeros((9, 64, 192), w.dtype)
    even = jnp.concatenate([w[:, 1], w[:, 0], zero, w[:, 2]], axis=1).reshape(5760, 192)
    odd = jnp.concatenate([w[:, 0], zero, w[:, 2], w[:, 1]], axis=1).reshape(5760, 192)
    return jnp.pad(even, ((0, 0), (0, 64))), jnp.pad(odd, ((0, 0), (64, 0)))


VMEM_SPEC = pl.BlockSpec(memory_space=pltpu.VMEM)


def local(latents, grid_slot, w_in, b_in, gain_in, w_up, b_up, gain_res, w_res, b_res):
    outbox = pl.pallas_call(
        outbox_kernel,
        out_shape=jax.ShapeDtypeStruct((1024, 128), BF16),
        in_specs=[VMEM_SPEC] * 2,
        out_specs=VMEM_SPEC,
        name="outbox",
    )(grid_slot.reshape(1, 128), latents)
    inbox = lax.all_to_all(
        outbox.reshape(128, 8, 128), ("seq", "tile"), split_axis=0, concat_axis=0, tiled=True
    )
    routed = pl.pallas_call(
        route_kernel,
        out_shape=jax.ShapeDtypeStruct((512, 128), BF16),
        in_specs=[VMEM_SPEC],
        out_specs=VMEM_SPEC,
        name="route",
    )(inbox.reshape(1024, 128))
    recv = lax.all_to_all(
        routed.reshape(8, 64, 128), "seq", split_axis=0, concat_axis=0, tiled=True
    ).reshape(512, 128)

    w0, wp = residual_weights(w_res)
    return pl.pallas_call(
        decode_kernel,
        out_shape=jax.ShapeDtypeStruct((16, 8, 6144), BF16),
        in_specs=[VMEM_SPEC] * 10,
        out_specs=VMEM_SPEC,
        scratch_shapes=[
            pltpu.VMEM((3, 8, 4, 16, 128), F32),
            pltpu.VMEM((8, 18, 16, 256), BF16),
            pltpu.VMEM((6, 18, 16, 384), BF16),
            pltpu.VMEM((10, 17, 16, 384), BF16),
            pltpu.VMEM((272, 768), F32),
            pltpu.VMEM((3, 10, 17, 16, 384), BF16),
            pltpu.VMEM((3, 2048, 128), F32),
        ],
        compiler_params=pltpu.CompilerParams(vmem_limit_bytes=56 * 1024 * 1024),
        name="decode",
    )(
        recv,
        first_weights(w_in),
        b_in.reshape(1, 384),
        gain_in.reshape(1, 384),
        corner_weights(w_up),
        jnp.tile(b_up, 2).reshape(1, 384),
        jnp.tile(gain_res, 2).reshape(1, 384),
        w0,
        wp,
        jnp.tile(b_res, 2).reshape(1, 384),
    )


def solution(mesh):
    return jax.shard_map(
        local,
        mesh=mesh,
        in_specs=(P(("seq", "tile"), None), P(("seq", "tile"))) + (P(),) * 8,
        out_specs=P(None, "tile", "seq"),
        check_vma=False,
    )
```

time: 624 us -> 104 us (0.17)
  the two profiles are of different devices: /device:TPU:7 before, /device:TPU:1 now
where the time goes in v1:
time: 104 us; the launch traced here: 103 us
  Pallas kernels  36.1 us (35%)
  other arithmetic  25.8 us (25%)
  local copies, waits for them, and re-layouts  24.6 us (24%)
  starting transfers between devices  16.8 us (16%)
    pallas_call x1, Pallas kernels, local(): pl.pallas_call(decode_kernel, out_shape=jax.ShapeDtypeStruct((16, 8, 6144...  31.8 us
    concatenate x1, other arithmetic, corner_weights(): return jnp.concatenate(blocks, axis=0).astype(BF16)  13.5 us
    all_to_all x1, starting transfers between devices, local(): lax.all_to_all(outbox.reshape(128, 8, 128), ('seq', 'tile'), split_axis=0...  12 us
    pad x2, local copies, waits for them, and re-layouts, residual_weights(): return (jnp.pad(even, ((0, 0), (0, 64))), jnp.pad(odd, ((0, 0), (64, 0))))  4.97 us
    all_to_all x1, starting transfers between devices, local(): lax.all_to_all(routed.reshape(8, 64, 128), 'seq', split_axis=0, concat_ax...  4.81 us
    unnamed x23, local copies, waits for them, and re-layouts  4.55 us
    add x2, local copies, waits for them, and re-layouts, corner_weights(): rows = [[w[0] + w[1], w[2]], [w[0], w[1] + w[2]]]  4.08 us
    another operation x2, other arithmetic  3.24 us
  transfers between devices with their start and end apart: 2, of which 0 were waited for; matrix products, arithmetic and copies ran while one was open for 48% of the time, Pallas kernels for 0%

profile of v1, /device:TPU:1, one launch (start us, length us, event | category | flops | bytes accessed | tf_op | source)
XLA Modules:
  0.0 103.4 jit_solution(10294660300873687243)
XLA Ops:
  0.0 2.0 %outbox.1 = bf16[1024,128]{1,0:T(8,128)(2,1)} custom-call(s32[1,128]{1,0:T(1,128)} %bitcast.73, bf16[128,128]{1,0:T(8,128)(2,1)} %lat_ref.1), custom_call_target="tpu_custom_call" | custom-call | tf_op jit(solution)/shard_map/outbox/pallas_call | solution.py:255
  2.0 12.0 %all-to-all-start = ((bf16[128,8,128]{2,1,0:T(8,128)(2,1)}), bf16[128,8,128]{2,1,0:T(8,128)(2,1)}, u32[]{:S(2)}, u32[]{:S(2)}) async-start(bf16[128,8,128]{2,1,0:T(8,128)(2,1)} %bitcast.69), calls=%async_computation | async-start | bytes 524288 | tf_op jit(solution)/shard_map/all_to_all | solution.py:262
  14.0 3.0 %convert_element_type.13 = f32[3456,192]{0,1:T(8,128)} convert(bf16[3456,192]{0,1:T(8,128)(2,1)} %param.15) | non-fusion elementwise | flops 663552 | bytes 3981312 | tf_op jit(solution)/shard_map/convert_element_type | solution.py:229
  17.0 2.5 %copy.20 = f32[3456,192]{1,0:T(8,128)S(1)} copy(bf16[3456,192]{0,1:T(8,128)(2,1)} %param.15) | data formatting | bytes 3981312 | tf_op jit(solution)/shard_map/convert_element_type | solution.py:229
  19.5 3.1 %slice_add_fusion.1 = (f32[1152,192]{0,1:T(8,128)}, f32[1152,192]{0,1:T(8,128)}) fusion(f32[3456,192]{0,1:T(8,128)} %convert_element_type.13), kind=kLoop, calls=%fused_computation.7 | loop fusion | flops 442368 | bytes 4423680 | tf_op jit(solution)/shard_map/add | solution.py:230
  22.6 2.5 %copy.19 = f32[1152,192]{1,0:T(8,128)} copy(f32[1152,192]{0,1:T(8,128)} %get-tuple-element.18) | data formatting | bytes 1769472 | tf_op jit(solution)/shard_map/add | solution.py:230
  25.2 2.2 %fusion = (bf16[384,192]{1,0:T(8,128)(2,1)}, bf16[384,192]{1,0:T(8,128)(2,1)}, bf16[384,192]{1,0:T(8,128)(2,1)}, bf16[384,192]{1,0:T(8,128)(2,1)}, bf16[384,192]{1,0:T(8,128)(2,1)}, /*index=5*/bf16[384,192]{1,0:T(8,128)(2,1)}) fusion(f32[1,3,384,192]{3,2,1,0:T(8,128)} %bitcast.65, f32[3,3,384,192]{3,2,1,0:T(8,128)S(1)} %bitcast.58), kind=kLoop, calls=%fused_computation.25 | loop fusion | bytes 1769472 | tf_op jit(solution)/shard_map/convert.16
  27.3 2.4 %fusion.8 = (bf16[384,192]{1,0:T(8,128)(2,1)}, bf16[384,192]{1,0:T(8,128)(2,1)}, bf16[384,192]{1,0:T(8,128)(2,1)}, bf16[384,192]{1,0:T(8,128)(2,1)}, bf16[384,192]{1,0:T(8,128)(2,1)}, /*index=5*/bf16[384,192]{1,0:T(8,128)(2,1)}) fusion(f32[1,3,384,192]{3,2,1,0:T(8,128)} %bitcast.66, f32[3,3,384,192]{3,2,1,0:T(8,128)S(1)} %bitcast.59), kind=kLoop, calls=%fused_computation.33 | loop fusion | flops 884736 | bytes 3538944 | tf_op jit(solution)/shard_map/convert.17
  29.7 1.5 %copy.21 = f32[1152,192]{1,0:T(8,128)S(1)} copy(f32[1152,192]{0,1:T(8,128)} %get-tuple-element.19) | data formatting | bytes 1769472 | tf_op jit(solution)/shard_map/add | solution.py:230
  31.3 0.0 copy-start
  31.3 0.8 fusion.5
  32.1 0.8 fusion.13
  32.9 3.8 %copy.22 = bf16[5184,192]{1,0:T(8,128)(2,1)S(1)} copy(bf16[5184,192]{0,1:T(8,128)(2,1)} %param.18) | data formatting | bytes 3981312 | tf_op args[8]
  36.8 13.5 %maximum_maximum_fusion.wc_ref = bf16[1536,768]{1,0:T(8,128)(2,1)} fusion(bf16[384,192]{1,0:T(8,128)(2,1)} %get-tuple-element.25, bf16[384,192]{1,0:T(8,128)(2,1)} %get-tuple-element.27, bf16[384,192]{1,0:T(8,128)(2,1)} %get-tuple-element.30, bf16[384,192]{1,0:T(8,128)(2,1)S(1)} %copy-done.3, bf16[384,192]{1,0:T(8,128)(2,1)} %get-tuple-element.26, ...), kind=kLoop, calls=%fused_computation.2 | loop fusion | flops 37748736 | bytes 4718592 | tf_op jit(solution)/shard_map/concatenate | solution.py:240
  50.3 1.4 %slice_bitcast_fusion.2 = (bf16[9,192,192]{2,1,0:T(8,128)(2,1)S(1)}, bf16[9,192,192]{2,1,0:T(8,128)(2,1)}, bf16[9,192,192]{2,1,0:T(8,128)(2,1)}) fusion(bf16[9,3,192,192]{3,2,1,0:T(8,128)(2,1)S(1)} %bitcast.62), kind=kLoop, calls=%fused_computation.5 | loop fusion | bytes 3981312 | tf_op jit(solution)/shard_map/squeeze | solution.py:246
  51.7 0.0 all-to-all-done
  51.8 2.3 %route.1 = bf16[512,128]{1,0:T(8,128)(2,1)} custom-call(bf16[1024,128]{1,0:T(8,128)(2,1)} %bitcast.2.inbox_ref), custom_call_target="tpu_custom_call" | custom-call | tf_op jit(solution)/shard_map/route/pallas_call | solution.py:265
  54.0 4.8 %all-to-all-start.1 = ((bf16[8,64,128]{2,1,0:T(8,128)(2,1)}), bf16[8,64,128]{2,1,0:T(8,128)(2,1)S(1)}, u32[]{:S(2)}, u32[]{:S(2)}) async-start(bf16[8,64,128]{2,1,0:T(8,128)(2,1)} %bitcast.71), calls=%async_computation.1 | async-start | bytes 262144 | tf_op jit(solution)/shard_map/all_to_all | solution.py:272
  58.8 2.9 %pad_maximum_fusion.1 = (bf16[9,640,192]{2,1,0:T(8,128)(2,1)S(1)}, bf16[9,640,192]{2,1,0:T(8,128)(2,1)S(1)}) fusion(bf16[9,192,192]{2,1,0:T(8,128)(2,1)S(1)} %get-tuple-element.15, bf16[9,192,192]{2,1,0:T(8,128)(2,1)} %get-tuple-element.16, bf16[9,64,192]{2,1,0:T(8,128)(2,1)S(1)} %broadcast_in_dim.3, bf16[9,192,192]{2,1,0:T(8,128)(2,1)} %get-tuple-element.17), kind=kLoop, calls=%fused_computation.1 | loop fusion | flops 17694720 | bytes 6635520 | tf_op jit(solution)/shard_map/concatenate | solution.py:247
  61.8 2.1 %pad.13.w0_ref = bf16[5760,256]{1,0:T(8,128)(2,1)} pad(bf16[5760,192]{1,0:T(8,128)(2,1)S(1)} %bitcast.61, bf16[]{:T(256)} %constant.1.clone.1), padding=0_0x0_64 | pad | bytes 5160962 | tf_op jit(solution)/shard_map/jit(_pad)/pad | solution.py:248
  63.9 0.0 copy-start.6
  63.9 0.0 copy-start.7
  63.9 2.9 %pad.14.wp_ref = bf16[5760,256]{1,0:T(8,128)(2,1)} pad(bf16[5760,192]{1,0:T(8,128)(2,1)S(1)} %bitcast.60, bf16[]{:T(256)} %constant.1.clone.1), padding=0_0x64_0 | pad | bytes 5160962 | tf_op jit(solution)/shard_map/jit(_pad)/pad | solution.py:248
  66.8 0.9 pad.12
  67.8 0.7 reshape_tile.10.g2_ref
  68.4 0.7 reshape_tile.11.b3_ref
  69.1 0.7 reshape_tile.9.bc_ref
  69.8 0.6 reshape.79.b1_ref
  70.4 0.6 reshape.80.g1_ref
  71.0 0.0 all-to-all-done.1
  71.0 0.7 copy-done.4
  71.6 31.8 %decode.1 = bf16[16,8,6144]{2,1,0:T(8,128)(2,1)} custom-call(bf16[512,128]{1,0:T(8,128)(2,1)} %bitcast.70, bf16[768,384]{1,0:T(8,128)(2,1)} %bitcast.67, f32[1,384]{1,0:T(1,128)} %reshape.79.b1_ref, f32[1,384]{1,0:T(1,128)} %reshape.80.g1_ref, bf16[1536,768]{1,0:T(8,128)(2,1)} %maximum_maximum_fusion.wc_ref, f32[1,384]{1,0:T(1,128)} %reshape_tile.9.bc_ref, ...), custom_call_target="tpu_custom_call" | custom-call | tf_op jit(solution)/shard_map/decode/pallas_call | solution.py:277
  (23 shorter events, 0.1 us)
Async XLA Ops:
  2.0 49.7 %all-to-all-start = ((bf16[128,8,128]{2,1,0:T(8,128)(2,1)}), bf16[128,8,128]{2,1,0:T(8,128)(2,1)}, u32[]{:S(2)}, u32[]{:S(2)}) async-start(bf16[128,8,128]{2,1,0:T(8,128)(2,1)} %bitcast.69), calls=%async_computation | async-start | bytes 524288 | tf_op jit(solution)/shard_map/all_to_all | solution.py:262
  31.3 5.5 %copy-start = (bf16[384,192]{1,0:T(8,128)(2,1)S(1)}, bf16[384,192]{1,0:T(8,128)(2,1)}, u32[]{:S(2)}) copy-start(bf16[384,192]{1,0:T(8,128)(2,1)} %get-tuple-element.22) | copy-start | bytes 442372
  31.3 5.5 %copy-start.1 = (bf16[384,192]{1,0:T(8,128)(2,1)S(1)}, bf16[384,192]{1,0:T(8,128)(2,1)}, u32[]{:S(2)}) copy-start(bf16[384,192]{1,0:T(8,128)(2,1)} %get-tuple-element.23) | copy-start | bytes 442372
  31.3 5.5 %copy-start.2 = (bf16[384,192]{1,0:T(8,128)(2,1)S(1)}, bf16[384,192]{1,0:T(8,128)(2,1)}, u32[]{:S(2)}) copy-start(bf16[384,192]{1,0:T(8,128)(2,1)} %get-tuple-element.32) | copy-start | bytes 442372
  31.3 5.5 %copy-start.3 = (bf16[384,192]{1,0:T(8,128)(2,1)S(1)}, bf16[384,192]{1,0:T(8,128)(2,1)}, u32[]{:S(2)}) copy-start(bf16[384,192]{1,0:T(8,128)(2,1)} %get-tuple-element.33) | copy-start | bytes 442372
  54.0 17.0 %all-to-all-start.1 = ((bf16[8,64,128]{2,1,0:T(8,128)(2,1)}), bf16[8,64,128]{2,1,0:T(8,128)(2,1)S(1)}, u32[]{:S(2)}, u32[]{:S(2)}) async-start(bf16[8,64,128]{2,1,0:T(8,128)(2,1)} %bitcast.71), calls=%async_computation.1 | async-start | bytes 262144 | tf_op jit(solution)/shard_map/all_to_all | solution.py:272
  63.8 3.0 %copy-start.5 = (bf16[432,384]{1,0:T(8,128)(2,1)S(1)}, bf16[432,384]{1,0:T(8,128)(2,1)}, u32[]{:S(2)}) copy-start(bf16[432,384]{1,0:T(8,128)(2,1)} %param.12) | copy-start | bytes 995332
  63.9 3.9 %copy-start.8 = (f32[192]{0:T(256)S(1)}, f32[192]{0:T(256)}, u32[]{:S(2)}) copy-start(f32[192]{0:T(256)} %param.17) | copy-start | bytes 2308
  63.9 4.6 %copy-start.9 = (f32[192]{0:T(256)S(1)}, f32[192]{0:T(256)}, u32[]{:S(2)}) copy-start(f32[192]{0:T(256)} %param.19) | copy-start | bytes 2308
  63.9 5.3 %copy-start.10 = (f32[192]{0:T(256)S(1)}, f32[192]{0:T(256)}, u32[]{:S(2)}) copy-start(f32[192]{0:T(256)} %param.16) | copy-start | bytes 2308
  63.9 5.9 %copy-start.6 = (f32[384]{0:T(512)S(1)}, f32[384]{0:T(512)}, u32[]{:S(2)}) copy-start(f32[384]{0:T(512)} %param.13) | copy-start | bytes 4612
  63.9 6.5 %copy-start.7 = (f32[384]{0:T(512)S(1)}, f32[384]{0:T(512)}, u32[]{:S(2)}) copy-start(f32[384]{0:T(512)} %param.14) | copy-start | bytes 4612
  71.0 0.7 copy-start.4

commit v2 on v1

--- a/solution.py
+++ b/solution.py
@@ -8,6 +8,7 @@
 F32 = jnp.float32
 BF16 = jnp.bfloat16
 I32 = jnp.int32
+MC = 2
 
 
 def iota(shape, dim):
@@ -72,17 +73,28 @@
     out_ref[...] = out.astype(BF16)
 
 
+def dot_nt(x, w):
+    return lax.dot_general(x, w, (((1,), (1,)), ((), ())), preferred_element_type=F32)
+
+
 def silu(v):
     half = 0.5 * v
     return half * jnp.tanh(half) + half
 
 
 def decode_kernel(
-    recv_ref, w1_ref, b1_ref, g1_ref, wc_ref, bc_ref, g2_ref, w0_ref, wp_ref, b3_ref,
-    out_ref, grid_ref, x_ref, a_ref, u_ref, acc_ref, r_ref, fin_ref,
+    recv_ref, w1_ref, wc_hbm, w0_hbm, wp_hbm, vec_ref, out_ref,
+    grid_ref, x_ref, a_ref, u_ref, r_ref, fin_ref, wc_ref, w0_ref, wp_ref, sems,
 ):
     s = lax.axis_index("seq")
     t = lax.axis_index("tile")
+    wc_copy = pltpu.make_async_copy(wc_hbm, wc_ref, sems.at[0])
+    w0_copy = pltpu.make_async_copy(w0_hbm, w0_ref, sems.at[1])
+    wp_copy = pltpu.make_async_copy(wp_hbm, wp_ref, sems.at[2])
+    wc_copy.start()
+    w0_copy.start()
+    wp_copy.start()
+    b1, g1, bc, g2, b3 = (vec_ref[n : n + 1, :] for n in range(5))
     lane = iota((1, 128), 1)
 
     i, k = iota((1536, 512), 0), iota((1536, 512), 1)
@@ -112,12 +124,12 @@
 
     def first(iy, carry):
         lhs = jnp.concatenate([x_ref[iy + d].reshape(288, 256) for d in range(3)], axis=1)
-        v = jnp.dot(lhs, w1_ref[...], preferred_element_type=F32) + b1_ref[...]
+        v = jnp.dot(lhs, w1_ref[...], preferred_element_type=F32) + b1
         scale = lax.rsqrt(jnp.mean(v * v, axis=1, keepdims=True) + 1e-06)
-        a_ref[iy] = silu(v * scale * g1_ref[...]).astype(BF16).reshape(18, 16, 384)
+        a_ref[iy] = silu(v * scale * g1).astype(BF16).reshape(18, 16, 384)
         return carry
 
-    lax.fori_loop(0, 6, first, 0)
+    lax.fori_loop(0, 6, first, 0, unroll=2)
 
     @pl.when(t == 0)
     def _():
@@ -134,15 +146,17 @@
     @pl.when(s == lax.axis_size("seq") - 1)
     def _():
         a_ref[:, 17] = jnp.zeros((6, 16, 384), BF16)
+
+    wc_copy.wait()
 
     def corners(ci, carry):
         lhs = jnp.concatenate(
             [a_ref[ci + d, pl.ds(e, 17)].reshape(272, 384) for d in range(2) for e in range(2)],
             axis=1,
         )
-        acc_ref[...] = jnp.dot(lhs, wc_ref[...], preferred_element_type=F32)
+        acc = dot_nt(lhs, wc_ref[...])
         for d in range(2):
-            u = (acc_ref[:, 384 * d : 384 * d + 384] + bc_ref[...]).astype(BF16)
+            u = (acc[:, 384 * d : 384 * d + 384] + bc).astype(BF16)
             u_ref[2 * ci + d] = u.reshape(17, 16, 384)
             u = u.astype(F32)
             sq = u * u
@@ -154,7 +168,7 @@
             low = jnp.broadcast_to(low, (272, 128))
             top = jnp.broadcast_to(top, (272, 128))
             scale = jnp.concatenate([low, jnp.where(lane < 64, low, top), top], axis=1)
-            r = silu(u * scale * g2_ref[...]).reshape(17, 16, 384)
+            r = silu(u * scale * g2).reshape(17, 16, 384)
             frame = iota((1, 16, 384), 1)
             r_ref[2, 2 * ci + d] = r.astype(BF16)
             for shift in (1, 2):
@@ -162,7 +176,7 @@
                 r_ref[2 - shift, 2 * ci + d] = moved.astype(BF16)
         return carry
 
-    lax.fori_loop(0, 5, corners, 0)
+    lax.fori_loop(0, 5, corners, 0, unroll=True)
 
     @pl.when(t == 0)
     def _():
@@ -186,69 +200,93 @@
         for d in range(3):
             r_ref[d, :, 16] = jnp.where(wide < 192, 0.0, r_ref[d, :, 16].astype(F32)).astype(BF16)
 
-    def residual(y, carry):
+    def residual(i, carry):
+        m = i * MC
+        R = MC * 128
         even, odd = [], []
         for d in range(3):
             for e in range(3):
-                even.append(r_ref[d, y + e, pl.ds(0, 16), :, :].reshape(256, 384))
-                even.append(r_ref[d, y + e, pl.ds(1, 16), :, 128:384].reshape(256, 256))
-                odd.append(r_ref[d, y + e, pl.ds(0, 16), :, 0:256].reshape(256, 256))
-                odd.append(r_ref[d, y + e, pl.ds(1, 16), :, :].reshape(256, 384))
-        p = jnp.dot(jnp.concatenate(even, axis=1), w0_ref[...], preferred_element_type=F32)
-        q = jnp.dot(jnp.concatenate(odd, axis=1), wp_ref[...], preferred_element_type=F32)
-        left = u_ref[y + 1, pl.ds(0, 16)].reshape(256, 384).astype(F32)
-        right = u_ref[y + 1, pl.ds(1, 16)].reshape(256, 384).astype(F32)
-        b3 = b3_ref[...]
-        at = pl.ds(pl.multiple_of(y * 256, 256), 256)
-        fin_ref[0, at, :] = p[:, 0:128] + b3[:, 0:128] + left[:, 0:128]
-        fin_ref[1, at, :] = (
-            p[:, 128:256] + q[:, 0:128] + b3[:, 128:256]
-            + jnp.where(lane < 64, left[:, 128:256], right[:, 128:256])
-        )
-        fin_ref[2, at, :] = q[:, 128:256] + b3[:, 256:384] + right[:, 256:384]
+                def tap(o, lo, hi):
+                    return jnp.concatenate([r_ref[d, pl.ds(e, 8), m + o + k, :, lo:hi].reshape(128, hi - lo) for k in range(MC)], axis=0)
+                even.append(tap(0, 0, 384)); even.append(tap(1, 128, 384))
+                odd.append(tap(0, 0, 256)); odd.append(tap(1, 0, 384))
+        p = dot_nt(jnp.concatenate(even, axis=1), w0_ref[...])
+        q = dot_nt(jnp.concatenate(odd, axis=1), wp_ref[...])
+        slot = i & 1
+        for k in range(MC):
+            left = u_ref[pl.ds(1, 8), m + k].reshape(128, 384).astype(F32)
+            right = u_ref[pl.ds(1, 8), m + k + 1].reshape(128, 384).astype(F32)
+            pk = p[128 * k : 128 * k + 128]
+            qk = q[128 * k : 128 * k + 128]
+            fin_ref[slot, k, 0] = pk[:, 0:128] + b3[:, 0:128] + left[:, 0:128]
+            fin_ref[slot, k, 1] = (
+                pk[:, 128:256] + qk[:, 0:128] + b3[:, 128:256]
+                + jnp.where(lane < 64, left[:, 128:256], right[:, 128:256])
+            )
+            fin_ref[slot, k, 2] = qk[:, 128:256] + b3[:, 256:384] + right[:, 256:384]
+        finish(i - 1, 1 - slot)
         return carry
 
-    lax.fori_loop(0, 8, residual, 0)
-
-    def finish(f, carry):
-        for m in range(16):
+    def finish(i, slot):
+        i = jnp.maximum(i, 0)
+        for k in range(MC):
             for c in range(3):
-                rows = fin_ref[c, pl.ds(m * 16 + f, 8, stride=256), :]
-                out_ref[f, :, 384 * m + 128 * c : 384 * m + 128 * c + 128] = rows.astype(BF16)
-        return carry
-
-    lax.fori_loop(0, 16, finish, 0)
-
-
-def first_weights(w_in):
-    w = w_in.reshape(3, 3, 48, 384).transpose(1, 0, 2, 3)
-    return jnp.pad(w, ((0, 0), (0, 1), (0, 16), (0, 0))).reshape(768, 384)
-
-
-def corner_weights(w_up):
-    w = w_up.reshape(3, 3, 384, 192).astype(F32)
-    rows = [[w[0] + w[1], w[2]], [w[0], w[1] + w[2]]]
-
-    def columns(v):
-        return [[v[0] + v[1], v[2]], [v[0], v[1] + v[2]]]
-
-    blocks = []
-    for r in range(2):
-        for c in range(2):
-            across = [columns(rows[dy][r])[dx][c] for dy in range(2) for dx in (1, 0)]
-            blocks.append(jnp.concatenate(across, axis=1))
-    return jnp.concatenate(blocks, axis=0).astype(BF16)
-
-
-def residual_weights(w_res):
-    w = w_res.reshape(9, 3, 192, 192)
-    zero = jnp.zeros((9, 64, 192), w.dtype)
-    even = jnp.concatenate([w[:, 1], w[:, 0], zero, w[:, 2]], axis=1).reshape(5760, 192)
-    odd = jnp.concatenate([w[:, 0], zero, w[:, 2], w[:, 1]], axis=1).reshape(5760, 192)
-    return jnp.pad(even, ((0, 0), (0, 64))), jnp.pad(odd, ((0, 0), (64, 0)))
+                for f in range(16):
+                    rows = fin_ref[slot, k, c, pl.ds(f, 8, stride=16), :]
+                    at = pl.multiple_of((i * MC + k) * 384 + c * 128, 128)
+                    out_ref[f, :, pl.ds(at, 128)] = rows.astype(BF16)
+
+    w0_copy.wait()
+    wp_copy.wait()
+    lax.fori_loop(0, 16 // MC, residual, 0)
+    finish(16 // MC - 1, (16 // MC - 1) & 1)
+
+
+def prepare_kernel(
+    win_ref, wup_ref, wres_ref, bin_ref, gin_ref, bup_ref, gres_ref, bres_ref,
+    w1_ref, wc_ref, w0_ref, wp_ref, vec_ref,
+):
+    for row in range(3):
+        for time in range(3):
+            at = row * 256 + time * 64
+            w1_ref[at : at + 48] = win_ref[(time * 3 + row) * 48 : (time * 3 + row) * 48 + 48]
+            w1_ref[at + 48 : at + 64] = jnp.zeros((16, 384), BF16)
+        w1_ref[row * 256 + 192 : row * 256 + 256] = jnp.zeros((64, 384), BF16)
+
+    taps = [[[0, 1], [2]], [[0], [1, 2]]]
+    for dy in range(2):
+        for place, dx in enumerate((1, 0)):
+            for r in range(2):
+                for c in range(2):
+                    total = None
+                    for b in taps[dy][r]:
+                        for e in taps[dx][c]:
+                            at = (b * 3 + e) * 384
+                            term = wup_ref[:, at : at + 384].astype(F32)
+                            total = term if total is None else total + term
+                    at = (r * 2 + c) * 384
+                    to = (dy * 2 + place) * 192
+                    wc_ref[to : to + 192, at : at + 384] = total.astype(BF16)
+
+    zero = jnp.zeros((192, 64), BF16)
+    for tap in range(9):
+        w = [wres_ref[:, (tap * 3 + e) * 192 : (tap * 3 + e) * 192 + 192] for e in range(3)]
+        at = slice(tap * 640, tap * 640 + 640)
+        w0_ref[0:192, at] = jnp.concatenate([w[1], w[0], zero, w[2]], axis=1)
+        wp_ref[64:256, at] = jnp.concatenate([w[0], zero, w[2], w[1]], axis=1)
+    w0_ref[192:256, :] = jnp.zeros((64, 5760), BF16)
+    wp_ref[0:64, :] = jnp.zeros((64, 5760), BF16)
+
+    vec_ref[...] = jnp.zeros((8, 384), F32)
+    for row, ref in enumerate((bin_ref, gin_ref)):
+        vec_ref[row : row + 1, :] = ref[...].reshape(1, 384)
+    for row, ref in enumerate((bup_ref, gres_ref, bres_ref)):
+        v = ref[...].reshape(1, 192)
+        vec_ref[row + 2 : row + 3, :] = jnp.concatenate([v, v], axis=1)
 
 
 VMEM_SPEC = pl.BlockSpec(memory_space=pltpu.VMEM)
+ANY_SPEC = pl.BlockSpec(memory_space=pl.ANY)
 
 
 def local(latents, grid_slot, w_in, b_in, gain_in, w_up, b_up, gain_res, w_res, b_res):
@@ -262,6 +300,21 @@
     inbox = lax.all_to_all(
         outbox.reshape(128, 8, 128), ("seq", "tile"), split_axis=0, concat_axis=0, tiled=True
     )
+    prepared = pl.pallas_call(
+        prepare_kernel,
+        out_shape=[
+            jax.ShapeDtypeStruct((768, 384), BF16),
+            jax.ShapeDtypeStruct((768, 1536), BF16),
+            jax.ShapeDtypeStruct((256, 5760), BF16),
+            jax.ShapeDtypeStruct((256, 5760), BF16),
+            jax.ShapeDtypeStruct((8, 384), F32),
+        ],
+        in_specs=[VMEM_SPEC] * 8,
+        out_specs=[VMEM_SPEC] * 5,
+        cost_estimate=pl.CostEstimate(flops=10_000_000, bytes_accessed=16_000_000, transcendentals=0),
+        compiler_params=pltpu.CompilerParams(vmem_limit_bytes=32 * 1024 * 1024),
+        name="prepare",
+    )(w_in, w_up.T, w_res.T, b_in, gain_in, b_up, gain_res, b_res)
     routed = pl.pallas_call(
         route_kernel,
         out_shape=jax.ShapeDtypeStruct((512, 128), BF16),
@@ -272,36 +325,30 @@
     recv = lax.all_to_all(
         routed.reshape(8, 64, 128), "seq", split_axis=0, concat_axis=0, tiled=True
     ).reshape(512, 128)
-
-    w0, wp = residual_weights(w_res)
+    return decode(recv, *prepared)
+
+
+def decode(recv, w1, wc, w0, wp, vec):
     return pl.pallas_call(
         decode_kernel,
         out_shape=jax.ShapeDtypeStruct((16, 8, 6144), BF16),
-        in_specs=[VMEM_SPEC] * 10,
+        in_specs=[VMEM_SPEC] * 2 + [ANY_SPEC] * 3 + [VMEM_SPEC],
         out_specs=VMEM_SPEC,
         scratch_shapes=[
             pltpu.VMEM((3, 8, 4, 16, 128), F32),
             pltpu.VMEM((8, 18, 16, 256), BF16),
             pltpu.VMEM((6, 18, 16, 384), BF16),
             pltpu.VMEM((10, 17, 16, 384), BF16),
-            pltpu.VMEM((272, 768), F32),
             pltpu.VMEM((3, 10, 17, 16, 384), BF16),
-            pltpu.VMEM((3, 2048, 128), F32),
+            pltpu.VMEM((2, MC, 3, 128, 128), F32),
+            pltpu.VMEM((768, 1536), BF16),
+            pltpu.VMEM((256, 5760), BF16),
+            pltpu.VMEM((256, 5760), BF16),
+            pltpu.SemaphoreType.DMA((3,)),
         ],
-        compiler_params=pltpu.CompilerParams(vmem_limit_bytes=56 * 1024 * 1024),
+        compiler_params=pltpu.CompilerParams(vmem_limit_bytes=48 * 1024 * 1024),
         name="decode",
-    )(
-        recv,
-        first_weights(w_in),
-        b_in.reshape(1, 384),
-        gain_in.reshape(1, 384),
-        corner_weights(w_up),
-        jnp.tile(b_up, 2).reshape(1, 384),
-        jnp.tile(gain_res, 2).reshape(1, 384),
-        w0,
-        wp,
-        jnp.tile(b_res, 2).reshape(1, 384),
-    )
+    )(recv, w1, wc, w0, wp, vec)
 
 
 def solution(mesh):

time: 104 us -> 72.9 us (0.70)
  other arithmetic: 25.8 us -> 0 us
  blocking collectives: 0 us -> 23.1 us
  local copies, waits for them, and re-layouts: 24.6 us -> 11.9 us
  starting transfers between devices: 16.8 us -> 4.36 us
  Pallas kernels: 36.1 us -> 32.9 us
    all_to_all x0 -> x1, blocking collectives: none -> 23.1 us  [local(): lax.all_to_all(outbox.reshape(128, 8, 128), ('seq', 'tile'), split_axis=0...]
    concatenate x2 -> x0, other arithmetic: 16.5 us -> none  [the longest x1 13.5 us: corner_weights(): return jnp.concatenate(blocks, axis=0).astype(BF16)]
    all_to_all x1 -> x0, starting transfers between devices: 12 us -> none  [local(): lax.all_to_all(outbox.reshape(128, 8, 128), ('seq', 'tile'), split_axis=0...]
    unnamed x23 -> x22, local copies, waits for them, and re-layouts: 4.55 us -> 11.9 us
    pad x3 -> x0, local copies, waits for them, and re-layouts: 5.91 us -> none  [the longest x2 4.97 us: residual_weights(): return (jnp.pad(even, ((0, 0), (0, 64))), jnp.pad(odd, ((0, 0), (64, 0))))]
    another operation x8 -> x0, local copies, waits for them, and re-layouts: 4.95 us -> none
    add x2 -> x0, local copies, waits for them, and re-layouts: 4.08 us -> none  [corner_weights(): rows = [[w[0] + w[1], w[2]], [w[0], w[1] + w[2]]]]
    another operation x2 -> x0, other arithmetic: 3.24 us -> none
  transfers between devices with their start and end apart: 2 -> 1, of which waited for: 0 -> 0; matrix products, arithmetic and copies ran while one was open for 48% -> 0% of each run, Pallas kernels for 0% -> 2%
where the time goes in v2:
time: 72.9 us; the launch traced here: 72.3 us
  Pallas kernels  32.9 us (45%)
  blocking collectives  23.1 us (32%)
  local copies, waits for them, and re-layouts  11.9 us (16%)
  starting transfers between devices  4.36 us (6%)
    pallas_call x1, Pallas kernels, decode(): pl.pallas_call(decode_kernel, out_shape=jax.ShapeDtypeStruct((16, 8, 6144...  26.9 us
    all_to_all x1, blocking collectives, local(): lax.all_to_all(outbox.reshape(128, 8, 128), ('seq', 'tile'), split_axis=0...  23.1 us
    unnamed x22, local copies, waits for them, and re-layouts  11.9 us
    all_to_all x1, starting transfers between devices, local(): lax.all_to_all(routed.reshape(8, 64, 128), 'seq', split_axis=0, concat_ax...  4.36 us
    pallas_call x1, Pallas kernels, local(): pl.pallas_call(route_kernel, out_shape=jax.ShapeDtypeStruct((512, 128), B...  2.25 us
    pallas_call x1, Pallas kernels, local(): pl.pallas_call(outbox_kernel, out_shape=jax.ShapeDtypeStruct((1024, 128),...  2.03 us
    pallas_call x1, Pallas kernels, local(): pl.pallas_call(prepare_kernel, out_shape=[jax.ShapeDtypeStruct((768, 384)...  1.74 us
  transfers between devices with their start and end apart: 1, of which 0 were waited for; matrix products, arithmetic and copies ran while one was open for 0% of the time, Pallas kernels for 2%

profile of v2, /device:TPU:1, one launch (start us, length us, event | category | flops | bytes accessed | tf_op | source)
XLA Modules:
  0.0 72.3 jit_solution(5105290413627985610)
XLA Ops:
  0.0 2.0 %outbox.1 = bf16[1024,128]{1,0:T(8,128)(2,1)} custom-call(s32[1,128]{1,0:T(1,128)} %bitcast.12, bf16[128,128]{1,0:T(8,128)(2,1)} %lat_ref.1), custom_call_target="tpu_custom_call" | custom-call | tf_op jit(solution)/shard_map/outbox/pallas_call | solution.py:293
  2.0 23.1 %all_to_all.10 = bf16[128,8,128]{2,1,0:T(8,128)(2,1)} all-to-all(bf16[128,8,128]{2,1,0:T(8,128)(2,1)} %bitcast.10), channel_id=1, replica_groups=mesh['seq'=8,'tile'=16] {'seq','tile'}, dimensions={0} | all-to-all | bytes 524288 | tf_op jit(solution)/shard_map/all_to_all | solution.py:300
  25.1 2.3 %route.1 = bf16[512,128]{1,0:T(8,128)(2,1)} custom-call(bf16[1024,128]{1,0:T(8,128)(2,1)} %bitcast.9), custom_call_target="tpu_custom_call" | custom-call | tf_op jit(solution)/shard_map/route/pallas_call | solution.py:318
  27.4 4.4 %all-to-all-start.1 = ((bf16[8,64,128]{2,1,0:T(8,128)(2,1)}), bf16[8,64,128]{2,1,0:T(8,128)(2,1)}, u32[]{:S(2)}, u32[]{:S(2)}) async-start(bf16[8,64,128]{2,1,0:T(8,128)(2,1)} %bitcast.11), calls=%async_computation.1 | async-start | bytes 262144 | tf_op jit(solution)/shard_map/all_to_all | solution.py:325
  31.7 0.0 copy-start.3
  31.7 1.6 %copy-done.3 = bf16[5184,192]{0,1:T(8,128)(2,1)S(1)} copy-done((bf16[5184,192]{0,1:T(8,128)(2,1)S(1)}, bf16[5184,192]{0,1:T(8,128)(2,1)}, u32[]{:S(2)}) %copy-start.3) | copy-done | bytes 1990680
  33.3 0.0 copy-start.4
  33.3 1.3 %copy-done.4 = bf16[3456,192]{0,1:T(8,128)(2,1)S(1)} copy-done((bf16[3456,192]{0,1:T(8,128)(2,1)S(1)}, bf16[3456,192]{0,1:T(8,128)(2,1)}, u32[]{:S(2)}) %copy-start.4) | copy-done | bytes 1327128
  34.6 0.0 copy-start.5
  34.6 1.0 %copy-done.5 = bf16[432,384]{1,0:T(8,128)(2,1)S(1)} copy-done((bf16[432,384]{1,0:T(8,128)(2,1)S(1)}, bf16[432,384]{1,0:T(8,128)(2,1)}, u32[]{:S(2)}) %copy-start.5) | copy-done | bytes 331800
  35.6 0.0 copy-start.6
  35.6 0.7 copy-done.6
  36.3 0.0 copy-start.7
  36.3 0.7 copy-done.7
  37.0 0.0 copy-start.8
  37.0 0.7 copy-done.8
  37.6 0.0 copy-start.9
  37.6 0.7 copy-done.9
  38.3 0.0 copy-start.10
  38.3 0.7 copy-done.10
  39.0 1.7 %prepare.1 = (bf16[768,384]{1,0:T(8,128)(2,1)S(1)}, bf16[768,1536]{1,0:T(8,128)(2,1)S(1)}, bf16[256,5760]{1,0:T(8,128)(2,1)S(1)}, bf16[256,5760]{1,0:T(8,128)(2,1)S(1)}, f32[8,384]{1,0:T(8,128)S(1)}) custom-call(bf16[432,384]{1,0:T(8,128)(2,1)S(1)} %copy-done.5, bf16[192,3456]{1,0:T(8,128)(2,1)S(1)} %bitcast.8, bf16[192,5184]{1,0:T(8,128)(2,1)S(1)} %bitcast.7, ...), custom_call_target="tpu_custom_call" | custom-call | flops 10000000 | bytes 16000000 | tf_op jit(solution)/shard_map/prepare/pallas_call | solution.py:303
  40.7 0.0 copy-start
  40.8 1.6 %copy-done = bf16[256,5760]{1,0:T(8,128)(2,1)} copy-done((bf16[256,5760]{1,0:T(8,128)(2,1)}, bf16[256,5760]{1,0:T(8,128)(2,1)S(1)}, u32[]{:S(2)}) %copy-start) | copy-done | bytes 2949144
  42.3 0.0 copy-start.1
  42.3 1.4 %copy-done.1 = bf16[768,1536]{1,0:T(8,128)(2,1)} copy-done((bf16[768,1536]{1,0:T(8,128)(2,1)}, bf16[768,1536]{1,0:T(8,128)(2,1)S(1)}, u32[]{:S(2)}) %copy-start.1) | copy-done | bytes 2359320
  43.8 0.0 all-to-all-done.1
  43.8 0.0 copy-start.2
  43.8 1.7 %copy-done.2 = bf16[768,1536]{1,0:T(8,128)(2,1)S(1)} copy-done((bf16[768,1536]{1,0:T(8,128)(2,1)S(1)}, bf16[768,1536]{1,0:T(8,128)(2,1)}, u32[]{:S(2)}) %copy-start.2) | copy-done | bytes 2359320
  45.4 26.9 %decode.1 = bf16[16,8,6144]{2,1,0:T(8,128)(2,1)} custom-call(bf16[512,128]{1,0:T(8,128)(2,1)} %bitcast.4.recv_ref, bf16[768,384]{1,0:T(8,128)(2,1)S(1)} %get-tuple-element.10.w1_ref, bf16[768,1536]{1,0:T(8,128)(2,1)S(1)} %copy-done.2, bf16[256,5760]{1,0:T(8,128)(2,1)S(1)} %get-tuple-element.12.w0_hbm, bf16[256,5760]{1,0:T(8,128)(2,1)} %copy-done, ...), custom_call_target="tpu_custom_call" | custom-call | tf_op jit(solution)/shard_map/decode/pallas_call | solution.py:332
Async XLA Ops:
  27.4 16.4 %all-to-all-start.1 = ((bf16[8,64,128]{2,1,0:T(8,128)(2,1)}), bf16[8,64,128]{2,1,0:T(8,128)(2,1)}, u32[]{:S(2)}, u32[]{:S(2)}) async-start(bf16[8,64,128]{2,1,0:T(8,128)(2,1)} %bitcast.11), calls=%async_computation.1 | async-start | bytes 262144 | tf_op jit(solution)/shard_map/all_to_all | solution.py:325
  31.7 1.6 %copy-start.3 = (bf16[5184,192]{0,1:T(8,128)(2,1)S(1)}, bf16[5184,192]{0,1:T(8,128)(2,1)}, u32[]{:S(2)}) copy-start(bf16[5184,192]{0,1:T(8,128)(2,1)} %param.18) | copy-start | bytes 5971972
  33.3 1.3 %copy-start.4 = (bf16[3456,192]{0,1:T(8,128)(2,1)S(1)}, bf16[3456,192]{0,1:T(8,128)(2,1)}, u32[]{:S(2)}) copy-start(bf16[3456,192]{0,1:T(8,128)(2,1)} %param.15) | copy-start | bytes 3981316
  34.6 1.0 %copy-start.5 = (bf16[432,384]{1,0:T(8,128)(2,1)S(1)}, bf16[432,384]{1,0:T(8,128)(2,1)}, u32[]{:S(2)}) copy-start(bf16[432,384]{1,0:T(8,128)(2,1)} %win_ref.1) | copy-start | bytes 995332
  35.6 0.7 copy-start.6
  36.3 0.7 copy-start.7
  37.0 0.7 copy-start.8
  37.6 0.7 copy-start.9
  38.3 0.7 copy-start.10
  40.7 1.6 %copy-start = (bf16[256,5760]{1,0:T(8,128)(2,1)}, bf16[256,5760]{1,0:T(8,128)(2,1)S(1)}, u32[]{:S(2)}) copy-start(bf16[256,5760]{1,0:T(8,128)(2,1)S(1)} %get-tuple-element.13.wp_hbm) | copy-start | bytes 8847364
  42.3 1.4 %copy-start.1 = (bf16[768,1536]{1,0:T(8,128)(2,1)}, bf16[768,1536]{1,0:T(8,128)(2,1)S(1)}, u32[]{:S(2)}) copy-start(bf16[768,1536]{1,0:T(8,128)(2,1)S(1)} %get-tuple-element.11.wc_hbm) | copy-start | bytes 7077892
  43.8 1.7 %copy-start.2 = (bf16[768,1536]{1,0:T(8,128)(2,1)S(1)}, bf16[768,1536]{1,0:T(8,128)(2,1)}, u32[]{:S(2)}) copy-start(bf16[768,1536]{1,0:T(8,128)(2,1)} %copy-done.1) | copy-start | bytes 7077892

commit v3 on v2

--- a/solution.py
+++ b/solution.py
@@ -56,7 +56,7 @@
     out_ref[...] = out.astype(BF16)
 
 
-def route_kernel(inbox_ref, out_ref):
+def route_kernel(inbox_ref, after_ref, out_ref):
     rows = inbox_ref.shape[0]
     inbox = inbox_ref[...]
     boxes = inbox.astype(F32).reshape(rows // 8, 8, 128)
@@ -146,6 +146,7 @@
     @pl.when(s == lax.axis_size("seq") - 1)
     def _():
         a_ref[:, 17] = jnp.zeros((6, 16, 384), BF16)
+
 
     wc_copy.wait()
 
@@ -243,16 +244,19 @@
 
 
 def prepare_kernel(
+    win_hbm, wup_hbm, wres_hbm, bin_hbm, gin_hbm, bup_hbm, gres_hbm, bres_hbm,
+    w1_ref, wc_hbm, w0_hbm, wp_hbm, vec_ref,
     win_ref, wup_ref, wres_ref, bin_ref, gin_ref, bup_ref, gres_ref, bres_ref,
-    w1_ref, wc_ref, w0_ref, wp_ref, vec_ref,
+    wc_ref, w0_ref, wp_ref, sems, out_sems,
 ):
-    for row in range(3):
-        for time in range(3):
-            at = row * 256 + time * 64
-            w1_ref[at : at + 48] = win_ref[(time * 3 + row) * 48 : (time * 3 + row) * 48 + 48]
-            w1_ref[at + 48 : at + 64] = jnp.zeros((16, 384), BF16)
-        w1_ref[row * 256 + 192 : row * 256 + 256] = jnp.zeros((64, 384), BF16)
-
+    pairs = (
+        (wup_hbm, wup_ref), (wres_hbm, wres_ref), (win_hbm, win_ref), (bin_hbm, bin_ref),
+        (gin_hbm, gin_ref), (bup_hbm, bup_ref), (gres_hbm, gres_ref), (bres_hbm, bres_ref),
+    )
+    copies = [pltpu.make_async_copy(x, y, sems.at[n]) for n, (x, y) in enumerate(pairs)]
+    for copy in copies:
+        copy.start()
+    copies[0].wait()
     taps = [[[0, 1], [2]], [[0], [1, 2]]]
     for dy in range(2):
         for place, dx in enumerate((1, 0)):
@@ -268,6 +272,9 @@
                     to = (dy * 2 + place) * 192
                     wc_ref[to : to + 192, at : at + 384] = total.astype(BF16)
 
+    wc_copy = pltpu.make_async_copy(wc_ref, wc_hbm, out_sems.at[0])
+    wc_copy.start()
+    copies[1].wait()
     zero = jnp.zeros((192, 64), BF16)
     for tap in range(9):
         w = [wres_ref[:, (tap * 3 + e) * 192 : (tap * 3 + e) * 192 + 192] for e in range(3)]
@@ -276,6 +283,19 @@
         wp_ref[64:256, at] = jnp.concatenate([w[0], zero, w[2], w[1]], axis=1)
     w0_ref[192:256, :] = jnp.zeros((64, 5760), BF16)
     wp_ref[0:64, :] = jnp.zeros((64, 5760), BF16)
+    w0_copy = pltpu.make_async_copy(w0_ref, w0_hbm, out_sems.at[1])
+    wp_copy = pltpu.make_async_copy(wp_ref, wp_hbm, out_sems.at[2])
+    w0_copy.start()
+    wp_copy.start()
+
+    for copy in copies[2:]:
+        copy.wait()
+    for row in range(3):
+        for time in range(3):
+            at = row * 256 + time * 64
+            w1_ref[at : at + 48] = win_ref[(time * 3 + row) * 48 : (time * 3 + row) * 48 + 48]
+            w1_ref[at + 48 : at + 64] = jnp.zeros((16, 384), BF16)
+        w1_ref[row * 256 + 192 : row * 256 + 256] = jnp.zeros((64, 384), BF16)
 
     vec_ref[...] = jnp.zeros((8, 384), F32)
     for row, ref in enumerate((bin_ref, gin_ref)):
@@ -283,10 +303,14 @@
     for row, ref in enumerate((bup_ref, gres_ref, bres_ref)):
         v = ref[...].reshape(1, 192)
         vec_ref[row + 2 : row + 3, :] = jnp.concatenate([v, v], axis=1)
+    wc_copy.wait()
+    w0_copy.wait()
+    wp_copy.wait()
 
 
 VMEM_SPEC = pl.BlockSpec(memory_space=pltpu.VMEM)
 ANY_SPEC = pl.BlockSpec(memory_space=pl.ANY)
+HBM_SPEC = pl.BlockSpec(memory_space=pltpu.HBM)
 
 
 def local(latents, grid_slot, w_in, b_in, gain_in, w_up, b_up, gain_res, w_res, b_res):
@@ -304,24 +328,45 @@
         prepare_kernel,
         out_shape=[
             jax.ShapeDtypeStruct((768, 384), BF16),
-            jax.ShapeDtypeStruct((768, 1536), BF16),
-            jax.ShapeDtypeStruct((256, 5760), BF16),
-            jax.ShapeDtypeStruct((256, 5760), BF16),
+            pltpu.HBM((768, 1536), BF16),
+            pltpu.HBM((256, 5760), BF16),
+            pltpu.HBM((256, 5760), BF16),
             jax.ShapeDtypeStruct((8, 384), F32),
         ],
-        in_specs=[VMEM_SPEC] * 8,
-        out_specs=[VMEM_SPEC] * 5,
+        in_specs=[HBM_SPEC] * 8,
+        out_specs=[VMEM_SPEC] + [HBM_SPEC] * 3 + [VMEM_SPEC],
+        scratch_shapes=[
+            pltpu.VMEM((432, 384), BF16),
+            pltpu.VMEM((192, 3456), BF16),
+            pltpu.VMEM((192, 5184), BF16),
+            pltpu.VMEM((384,), F32),
+            pltpu.VMEM((384,), F32),
+            pltpu.VMEM((192,), F32),
+            pltpu.VMEM((192,), F32),
+            pltpu.VMEM((192,), F32),
+            pltpu.VMEM((768, 1536), BF16),
+            pltpu.VMEM((256, 5760), BF16),
+            pltpu.VMEM((256, 5760), BF16),
+            pltpu.SemaphoreType.DMA((8,)),
+            pltpu.SemaphoreType.DMA((3,)),
+        ],
         cost_estimate=pl.CostEstimate(flops=10_000_000, bytes_accessed=16_000_000, transcendentals=0),
-        compiler_params=pltpu.CompilerParams(vmem_limit_bytes=32 * 1024 * 1024),
+        compiler_params=pltpu.CompilerParams(vmem_limit_bytes=28 * 1024 * 1024),
         name="prepare",
-    )(w_in, w_up.T, w_res.T, b_in, gain_in, b_up, gain_res, b_res)
+    )(
+        *(
+            pltpu.with_memory_space_constraint(w, pltpu.HBM)
+            for w in (w_in, w_up.T, w_res.T, b_in, gain_in, b_up, gain_res, b_res)
+        )
+    )
     routed = pl.pallas_call(
         route_kernel,
         out_shape=jax.ShapeDtypeStruct((512, 128), BF16),
-        in_specs=[VMEM_SPEC],
+        in_specs=[VMEM_SPEC, ANY_SPEC],
         out_specs=VMEM_SPEC,
+        compiler_params=pltpu.CompilerParams(vmem_limit_bytes=12 * 1024 * 1024),
         name="route",
-    )(inbox.reshape(1024, 128))
+    )(inbox.reshape(1024, 128), prepared[4])
     recv = lax.all_to_all(
         routed.reshape(8, 64, 128), "seq", split_axis=0, concat_axis=0, tiled=True
     ).reshape(512, 128)
@@ -332,7 +377,7 @@
     return pl.pallas_call(
         decode_kernel,
         out_shape=jax.ShapeDtypeStruct((16, 8, 6144), BF16),
-        in_specs=[VMEM_SPEC] * 2 + [ANY_SPEC] * 3 + [VMEM_SPEC],
+        in_specs=[VMEM_SPEC] * 2 + [HBM_SPEC] * 3 + [VMEM_SPEC],
         out_specs=VMEM_SPEC,
         scratch_shapes=[
             pltpu.VMEM((3, 8, 4, 16, 128), F32),
@@ -346,9 +391,9 @@
             pltpu.VMEM((256, 5760), BF16),
             pltpu.SemaphoreType.DMA((3,)),
         ],
-        compiler_params=pltpu.CompilerParams(vmem_limit_bytes=48 * 1024 * 1024),
+        compiler_params=pltpu.CompilerParams(vmem_limit_bytes=44 * 1024 * 1024),
         name="decode",
-    )(recv, w1, wc, w0, wp, vec)
+    )(recv, w1, *(pltpu.with_memory_space_constraint(w, pltpu.HBM) for w in (wc, w0, wp)), vec)
 
 
 def solution(mesh):

time: 72.9 us -> 59.6 us (0.82)
  blocking collectives: 23.1 us -> 8.14 us
  local copies, waits for them, and re-layouts: 11.9 us -> 0 us
  starting transfers between devices: 4.36 us -> 11.5 us
  waiting for transfers between devices: 0.01 us -> 6.07 us
    all_to_all x1, blocking collectives: 23.1 us -> 8.14 us  [local(): lax.all_to_all(routed.reshape(8, 64, 128), 'seq', split_axis=0, concat_ax...]
    unnamed x22 -> x0, local copies, waits for them, and re-layouts: 11.9 us -> none
    all_to_all x1, starting transfers between devices: 4.36 us -> 11.5 us  [local(): lax.all_to_all(outbox.reshape(128, 8, 128), ('seq', 'tile'), split_axis=0...]
    all_to_all x1, waiting for transfers between devices: 0.01 us -> 6.07 us  [local(): lax.all_to_all(outbox.reshape(128, 8, 128), ('seq', 'tile'), split_axis=0...]
    pallas_call x1, Pallas kernels: 1.74 us -> 5.39 us  [local(): pl.pallas_call(prepare_kernel, out_shape=[jax.ShapeDtypeStruct((768, 384)...]
    pallas_call x1, Pallas kernels: 2.25 us -> 0.65 us  [local(): pl.pallas_call(route_kernel, out_shape=jax.ShapeDtypeStruct((512, 128), B...]
    pallas_call x1, Pallas kernels: 26.9 us -> 25.5 us  [decode(): pl.pallas_call(decode_kernel, out_shape=jax.ShapeDtypeStruct((16, 8, 6144...]
  transfers between devices with their start and end apart: 1 -> 1, of which waited for: 0 -> 1; matrix products, arithmetic and copies ran while one was open for 0% -> 0% of each run, Pallas kernels for 2% -> 9%
where the time goes in v3:
time: 59.6 us; the launch traced here: 59.3 us
  Pallas kernels  33.6 us (56%)
  starting transfers between devices  11.5 us (19%)
  blocking collectives  8.14 us (14%)
  waiting for transfers between devices  6.07 us (10%)
    pallas_call x1, Pallas kernels, decode(): pl.pallas_call(decode_kernel, out_shape=jax.ShapeDtypeStruct((16, 8, 6144...  25.5 us
    all_to_all x1, starting transfers between devices, local(): lax.all_to_all(outbox.reshape(128, 8, 128), ('seq', 'tile'), split_axis=0...  11.5 us
    all_to_all x1, blocking collectives, local(): lax.all_to_all(routed.reshape(8, 64, 128), 'seq', split_axis=0, concat_ax...  8.14 us
    all_to_all x1, waiting for transfers between devices, local(): lax.all_to_all(outbox.reshape(128, 8, 128), ('seq', 'tile'), split_axis=0...  6.07 us
    pallas_call x1, Pallas kernels, local(): pl.pallas_call(prepare_kernel, out_shape=[jax.ShapeDtypeStruct((768, 384)...  5.39 us
    pallas_call x1, Pallas kernels, local(): pl.pallas_call(outbox_kernel, out_shape=jax.ShapeDtypeStruct((1024, 128),...  2.03 us
  transfers between devices with their start and end apart: 1, of which 1 were waited for; matrix products, arithmetic and copies ran while one was open for 0% of the time, Pallas kernels for 9%

profile of v3, /device:TPU:1, one launch (start us, length us, event | category | flops | bytes accessed | tf_op | source)
XLA Modules:
  0.0 59.3 jit_solution(3846541344265242876)
XLA Ops:
  0.0 2.0 %outbox.1 = bf16[1024,128]{1,0:T(8,128)(2,1)} custom-call(s32[1,128]{1,0:T(1,128)} %bitcast.13, bf16[128,128]{1,0:T(8,128)(2,1)} %lat_ref.1), custom_call_target="tpu_custom_call" | custom-call | tf_op jit(solution)/shard_map/outbox/pallas_call | solution.py:317
  2.0 11.5 %all-to-all-start = ((bf16[128,8,128]{2,1,0:T(8,128)(2,1)}), bf16[128,8,128]{2,1,0:T(8,128)(2,1)S(1)}, u32[]{:S(2)}, u32[]{:S(2)}) async-start(bf16[128,8,128]{2,1,0:T(8,128)(2,1)} %bitcast.12), calls=%async_computation | async-start | bytes 524288 | tf_op jit(solution)/shard_map/all_to_all | solution.py:324
  13.5 5.4 %prepare.1 = (bf16[768,384]{1,0:T(8,128)(2,1)S(1)}, bf16[768,1536]{1,0:T(8,128)(2,1)}, bf16[256,5760]{1,0:T(8,128)(2,1)}, bf16[256,5760]{1,0:T(8,128)(2,1)}, f32[8,384]{1,0:T(8,128)S(1)}) custom-call(bf16[432,384]{1,0:T(8,128)(2,1)} %win_hbm.1, bf16[192,3456]{1,0:T(8,128)(2,1)} %bitcast.11, bf16[192,5184]{1,0:T(8,128)(2,1)} %bitcast.10, f32[384]{0:T(512)} %bin_hbm.1, ...), custom_call_target="tpu_custom_call" | custom-call | flops 10000000 | bytes 16000000 | tf_op jit(solution)/shard_map/prepare/pallas_call | solution.py:327
  18.9 6.1 %all-to-all-done = bf16[128,8,128]{2,1,0:T(8,128)(2,1)S(1)} async-done(((bf16[128,8,128]{2,1,0:T(8,128)(2,1)}), bf16[128,8,128]{2,1,0:T(8,128)(2,1)S(1)}, u32[]{:S(2)}, u32[]{:S(2)}) %all-to-all-start) | async-done | bytes 262176 | tf_op jit(solution)/shard_map/all_to_all | solution.py:324
  25.0 0.6 %route.1 = bf16[512,128]{1,0:T(8,128)(2,1)S(1)} custom-call(bf16[1024,128]{1,0:T(8,128)(2,1)S(1)} %bitcast.7, f32[8,384]{1,0:T(8,128)S(1)} %get-tuple-element.10.after_ref.vec_ref), custom_call_target="tpu_custom_call" | custom-call | tf_op jit(solution)/shard_map/route/pallas_call | solution.py:362
  25.7 8.1 %all_to_all.10 = bf16[8,64,128]{2,1,0:T(8,128)(2,1)S(1)} all-to-all(bf16[8,64,128]{2,1,0:T(8,128)(2,1)S(1)} %bitcast.9), channel_id=1, replica_groups=mesh['seq'=8,'tile'=16] {'seq'}, dimensions={0} | all-to-all | bytes 262144 | tf_op jit(solution)/shard_map/all_to_all | solution.py:370
  33.8 25.5 %decode.1 = bf16[16,8,6144]{2,1,0:T(8,128)(2,1)} custom-call(bf16[512,128]{1,0:T(8,128)(2,1)S(1)} %bitcast.8, bf16[768,384]{1,0:T(8,128)(2,1)S(1)} %get-tuple-element.11.w1_ref, bf16[768,1536]{1,0:T(8,128)(2,1)} %get-tuple-element.12.wc_hbm, bf16[256,5760]{1,0:T(8,128)(2,1)} %get-tuple-element.13.w0_hbm, bf16[256,5760]{1,0:T(8,128)(2,1)} %get-tuple-element.14.wp_hbm, ...), custom_call_target="tpu_custom_call" | custom-call | tf_op jit(solution)/shard_map/decode/pallas_call | solution.py:377
Async XLA Ops:
  2.0 23.0 %all-to-all-start = ((bf16[128,8,128]{2,1,0:T(8,128)(2,1)}), bf16[128,8,128]{2,1,0:T(8,128)(2,1)S(1)}, u32[]{:S(2)}, u32[]{:S(2)}) async-start(bf16[128,8,128]{2,1,0:T(8,128)(2,1)} %bitcast.12), calls=%async_computation | async-start | bytes 524288 | tf_op jit(solution)/shard_map/all_to_all | solution.py:324

commit v4 on v3

--- a/solution.py
+++ b/solution.py
@@ -8,7 +8,7 @@
 F32 = jnp.float32
 BF16 = jnp.bfloat16
 I32 = jnp.int32
-MC = 2
+NI = 8
 
 
 def iota(shape, dim):
@@ -90,7 +90,7 @@
     t = lax.axis_index("tile")
     wc_copy = pltpu.make_async_copy(wc_hbm, wc_ref, sems.at[0])
     w0_copy = pltpu.make_async_copy(w0_hbm, w0_ref, sems.at[1])
-    wp_copy = pltpu.make_async_copy(wp_hbm, wp_ref, sems.at[2])
+    wp_copy = pltpu.make_async_copy(wp_hbm, wp_ref.at[pl.ds(64, 192)], sems.at[2])
     wc_copy.start()
     w0_copy.start()
     wp_copy.start()
@@ -98,7 +98,7 @@
     lane = iota((1, 128), 1)
 
     i, k = iota((1536, 512), 0), iota((1536, 512), 1)
-    key_i = ((i >> 4) & 31) * 32 + (i & 15) - 2 + (i >> 9)
+    key_i = ((i >> 4) & 31) * 32 + 2 * (i & 7) + ((i >> 3) & 1) - 2 + (i >> 9)
     key_k = ((k >> 1) & 31) * 32 + 2 * (k >> 6) + (k & 1)
     grid_ref[...] = jnp.dot(
         ones_where(key_i == key_k), recv_ref[...], preferred_element_type=F32
@@ -170,77 +170,101 @@
             top = jnp.broadcast_to(top, (272, 128))
             scale = jnp.concatenate([low, jnp.where(lane < 64, low, top), top], axis=1)
             r = silu(u * scale * g2).reshape(17, 16, 384)
-            frame = iota((1, 16, 384), 1)
-            r_ref[2, 2 * ci + d] = r.astype(BF16)
-            for shift in (1, 2):
-                moved = jnp.where(frame >= shift, pltpu.roll(r, shift, 1), 0.0)
-                r_ref[2 - shift, 2 * ci + d] = moved.astype(BF16)
+            d2, d3 = r[:, 0:8], r[:, 8:16]
+            later = iota((1, 8, 384), 1) > 0
+            d0 = jnp.where(later, pltpu.roll(d2, 1, 1), 0.0)
+            d1 = jnp.where(later, pltpu.roll(d3, 1, 1), 0.0)
+            for n, v in enumerate((d0 - d2, d1 + d2, d2 - d1, d1 - d3)):
+                r_ref[n, 0, 2 * ci + d] = v[0:16].reshape(8, 16, 384).astype(BF16)
+                r_ref[n, 1, 2 * ci + d] = v[1:17].reshape(8, 16, 384).astype(BF16)
         return carry
 
     lax.fori_loop(0, 5, corners, 0, unroll=True)
 
     @pl.when(t == 0)
     def _():
-        for d in range(3):
-            r_ref[d, 0] = jnp.zeros((17, 16, 384), BF16)
+        for n in range(4):
+            r_ref[n, :, 0] = jnp.zeros((2, 8, 16, 384), BF16)
 
     @pl.when(t == lax.axis_size("tile") - 1)
     def _():
-        for d in range(3):
-            r_ref[d, 9] = jnp.zeros((17, 16, 384), BF16)
-
-    wide = iota((1, 1, 384), 2)
+        for n in range(4):
+            r_ref[n, :, 9] = jnp.zeros((2, 8, 16, 384), BF16)
+
+    row, wide = iota((1, 16, 384), 1), iota((1, 16, 384), 2)
 
     @pl.when(s == 0)
     def _():
-        for d in range(3):
-            r_ref[d, :, 0] = jnp.where(wide < 192, r_ref[d, :, 0].astype(F32), 0.0).astype(BF16)
+        for n in range(4):
+            v = r_ref[n, 0, :, 0].astype(F32)
+            r_ref[n, 0, :, 0] = jnp.where((wide < 192) | (row >= 8), v, 0.0).astype(BF16)
 
     @pl.when(s == lax.axis_size("seq") - 1)
     def _():
-        for d in range(3):
-            r_ref[d, :, 16] = jnp.where(wide < 192, 0.0, r_ref[d, :, 16].astype(F32)).astype(BF16)
+        for n in range(4):
+            v = r_ref[n, 1, :, 7].astype(F32)
+            r_ref[n, 1, :, 7] = jnp.where((wide >= 192) | (row < 8), v, 0.0).astype(BF16)
 
     def residual(i, carry):
-        m = i * MC
-        R = MC * 128
         even, odd = [], []
-        for d in range(3):
+        for n in range(4):
+            pieces = [[], []]
             for e in range(3):
-                def tap(o, lo, hi):
-                    return jnp.concatenate([r_ref[d, pl.ds(e, 8), m + o + k, :, lo:hi].reshape(128, hi - lo) for k in range(MC)], axis=0)
-                even.append(tap(0, 0, 384)); even.append(tap(1, 128, 384))
-                odd.append(tap(0, 0, 256)); odd.append(tap(1, 0, 384))
-        p = dot_nt(jnp.concatenate(even, axis=1), w0_ref[...])
-        q = dot_nt(jnp.concatenate(odd, axis=1), wp_ref[...])
+                def tap(shift, low, high):
+                    return jnp.concatenate(
+                        [
+                            r_ref[n, shift, pl.ds(e, 8), i * NI + k, :, low:high].reshape(128, high - low)
+                            for k in range(NI)
+                        ],
+                        axis=0,
+                    )
+
+                pieces[0] += [tap(0, 0, 384), tap(1, 128, 384)]
+                pieces[1] += [tap(0, 0, 256), tap(1, 0, 384)]
+            at = slice(n * 1920, n * 1920 + 1920)
+            even.append(dot_nt(jnp.concatenate(pieces[0], axis=1), w0_ref[:, at]))
+            odd.append(dot_nt(jnp.concatenate(pieces[1], axis=1), wp_ref[:, at]))
         slot = i & 1
-        for k in range(MC):
-            left = u_ref[pl.ds(1, 8), m + k].reshape(128, 384).astype(F32)
-            right = u_ref[pl.ds(1, 8), m + k + 1].reshape(128, 384).astype(F32)
-            pk = p[128 * k : 128 * k + 128]
-            qk = q[128 * k : 128 * k + 128]
-            fin_ref[slot, k, 0] = pk[:, 0:128] + b3[:, 0:128] + left[:, 0:128]
-            fin_ref[slot, k, 1] = (
-                pk[:, 128:256] + qk[:, 0:128] + b3[:, 128:256]
-                + jnp.where(lane < 64, left[:, 128:256], right[:, 128:256])
-            )
-            fin_ref[slot, k, 2] = qk[:, 128:256] + b3[:, 256:384] + right[:, 256:384]
+        for parity in range(2):
+            if parity == 0:
+                p, q = (v[0] + (v[1] + v[2]) for v in (even, odd))
+            else:
+                p, q = (v[1] - v[2] - v[3] for v in (even, odd))
+            p = p.reshape(NI, 8, 2, 8, 192)
+            q = q.reshape(NI, 8, 2, 8, 256)
+            for k in range(NI):
+                for c in range(2):
+                    m = (i * NI + k) * 2 + c
+                    pk, qk = p[k, :, c], q[k, :, c]
+                    now = slice(8 * parity, 8 * parity + 8)
+                    left = u_ref[pl.ds(1, 8), m].astype(F32)[:, now]
+                    right = u_ref[pl.ds(1, 8), m + 1].astype(F32)[:, now]
+                    mid = jnp.where(lane < 64, left[..., 128:256], right[..., 128:256])
+                    edge = jnp.concatenate([pk[..., 128:192], jnp.zeros((8, 8, 64), F32)], axis=2)
+                    parts = (
+                        pk[..., 0:128] + b3[:, 0:128] + left[..., 0:128],
+                        edge + qk[..., 0:128] + b3[:, 128:256] + mid,
+                        qk[..., 128:256] + b3[:, 256:384] + right[..., 256:384],
+                    )
+                    for z, part in enumerate(parts):
+                        fin_ref[slot, 2 * k + c, parity, z] = part.reshape(64, 128)
         finish(i - 1, 1 - slot)
         return carry
 
     def finish(i, slot):
         i = jnp.maximum(i, 0)
-        for k in range(MC):
+        for k in range(2 * NI):
             for c in range(3):
                 for f in range(16):
-                    rows = fin_ref[slot, k, c, pl.ds(f, 8, stride=16), :]
-                    at = pl.multiple_of((i * MC + k) * 384 + c * 128, 128)
+                    rows = fin_ref[slot, k, f & 1, c, pl.ds(f >> 1, 8, stride=8), :]
+                    at = pl.multiple_of((i * 2 * NI + k) * 384 + c * 128, 128)
                     out_ref[f, :, pl.ds(at, 128)] = rows.astype(BF16)
 
+    wp_ref[0:64, :] = jnp.zeros((64, 7680), BF16)
     w0_copy.wait()
     wp_copy.wait()
-    lax.fori_loop(0, 16 // MC, residual, 0)
-    finish(16 // MC - 1, (16 // MC - 1) & 1)
+    lax.fori_loop(0, 8 // NI, residual, 0)
+    finish(8 // NI - 1, (8 // NI - 1) & 1)
 
 
 def prepare_kernel(
@@ -276,13 +300,16 @@
     wc_copy.start()
     copies[1].wait()
     zero = jnp.zeros((192, 64), BF16)
-    for tap in range(9):
-        w = [wres_ref[:, (tap * 3 + e) * 192 : (tap * 3 + e) * 192 + 192] for e in range(3)]
-        at = slice(tap * 640, tap * 640 + 640)
-        w0_ref[0:192, at] = jnp.concatenate([w[1], w[0], zero, w[2]], axis=1)
-        wp_ref[64:256, at] = jnp.concatenate([w[0], zero, w[2], w[1]], axis=1)
-    w0_ref[192:256, :] = jnp.zeros((64, 5760), BF16)
-    wp_ref[0:64, :] = jnp.zeros((64, 5760), BF16)
+    for row in range(3):
+        g = [wres_ref[:, (time * 3 + row) * 576 : (time * 3 + row) * 576 + 576] for time in range(3)]
+        ends = (g[0].astype(F32) + g[2].astype(F32)) * 0.5
+        mid = g[1].astype(F32) * 0.5
+        taps = (g[0], (ends + mid).astype(BF16), (ends - mid).astype(BF16), g[2])
+        for n, tap in enumerate(taps):
+            w = [tap[:, e * 192 : e * 192 + 192] for e in range(3)]
+            at = slice(n * 1920 + row * 640, n * 1920 + row * 640 + 640)
+            w0_ref[:, at] = jnp.concatenate([w[1], w[0], zero, w[2]], axis=1)
+            wp_ref[:, at] = jnp.concatenate([w[0], zero, w[2], w[1]], axis=1)
     w0_copy = pltpu.make_async_copy(w0_ref, w0_hbm, out_sems.at[1])
     wp_copy = pltpu.make_async_copy(wp_ref, wp_hbm, out_sems.at[2])
     w0_copy.start()
@@ -329,8 +356,8 @@
         out_shape=[
             jax.ShapeDtypeStruct((768, 384), BF16),
             pltpu.HBM((768, 1536), BF16),
-            pltpu.HBM((256, 5760), BF16),
-            pltpu.HBM((256, 5760), BF16),
+            pltpu.HBM((192, 7680), BF16),
+            pltpu.HBM((192, 7680), BF16),
             jax.ShapeDtypeStruct((8, 384), F32),
         ],
         in_specs=[HBM_SPEC] * 8,
@@ -345,8 +372,8 @@
             pltpu.VMEM((192,), F32),
             pltpu.VMEM((192,), F32),
             pltpu.VMEM((768, 1536), BF16),
-            pltpu.VMEM((256, 5760), BF16),
-            pltpu.VMEM((256, 5760), BF16),
+            pltpu.VMEM((192, 7680), BF16),
+            pltpu.VMEM((192, 7680), BF16),
             pltpu.SemaphoreType.DMA((8,)),
             pltpu.SemaphoreType.DMA((3,)),
         ],
@@ -384,11 +411,11 @@
             pltpu.VMEM((8, 18, 16, 256), BF16),
             pltpu.VMEM((6, 18, 16, 384), BF16),
             pltpu.VMEM((10, 17, 16, 384), BF16),
-            pltpu.VMEM((3, 10, 17, 16, 384), BF16),
-            pltpu.VMEM((2, MC, 3, 128, 128), F32),
+            pltpu.VMEM((4, 2, 10, 8, 16, 384), BF16),
+            pltpu.VMEM((2, 2 * NI, 2, 3, 64, 128), F32),
             pltpu.VMEM((768, 1536), BF16),
-            pltpu.VMEM((256, 5760), BF16),
-            pltpu.VMEM((256, 5760), BF16),
+            pltpu.VMEM((192, 7680), BF16),
+            pltpu.VMEM((256, 7680), BF16),
             pltpu.SemaphoreType.DMA((3,)),
         ],
         compiler_params=pltpu.CompilerParams(vmem_limit_bytes=44 * 1024 * 1024),

time: 59.6 us -> 54.1 us (0.908)
  Pallas kernels: 33.6 us -> 28.5 us
    pallas_call x1, Pallas kernels: 25.5 us -> 19.9 us  [decode(): pl.pallas_call(decode_kernel, out_shape=jax.ShapeDtypeStruct((16, 8, 6144...]
  transfers between devices with their start and end apart: 1 -> 1, of which waited for: 1 -> 1; matrix products, arithmetic and copies ran while one was open for 0% -> 0% of each run, Pallas kernels for 9% -> 11%
where the time goes in v4:
time: 54.1 us; the launch traced here: 53.8 us
  Pallas kernels  28.5 us (53%)
  starting transfers between devices  11.5 us (21%)
  blocking collectives  8.14 us (15%)
  waiting for transfers between devices  5.53 us (10%)
    pallas_call x1, Pallas kernels, decode(): pl.pallas_call(decode_kernel, out_shape=jax.ShapeDtypeStruct((16, 8, 6144...  19.9 us
    all_to_all x1, starting transfers between devices, local(): lax.all_to_all(outbox.reshape(128, 8, 128), ('seq', 'tile'), split_axis=0...  11.5 us
    all_to_all x1, blocking collectives, local(): lax.all_to_all(routed.reshape(8, 64, 128), 'seq', split_axis=0, concat_ax...  8.14 us
    pallas_call x1, Pallas kernels, local(): pl.pallas_call(prepare_kernel, out_shape=[jax.ShapeDtypeStruct((768, 384)...  5.93 us
    all_to_all x1, waiting for transfers between devices, local(): lax.all_to_all(outbox.reshape(128, 8, 128), ('seq', 'tile'), split_axis=0...  5.53 us
    pallas_call x1, Pallas kernels, local(): pl.pallas_call(outbox_kernel, out_shape=jax.ShapeDtypeStruct((1024, 128),...  2.04 us
  transfers between devices with their start and end apart: 1, of which 1 were waited for; matrix products, arithmetic and copies ran while one was open for 0% of the time, Pallas kernels for 11%

profile of v4, /device:TPU:1, one launch (start us, length us, event | category | flops | bytes accessed | tf_op | source)
XLA Modules:
  0.0 53.8 jit_solution(6115357221107375010)
XLA Ops:
  0.0 2.0 %outbox.1 = bf16[1024,128]{1,0:T(8,128)(2,1)} custom-call(s32[1,128]{1,0:T(1,128)} %bitcast.13, bf16[128,128]{1,0:T(8,128)(2,1)} %lat_ref.1), custom_call_target="tpu_custom_call" | custom-call | tf_op jit(solution)/shard_map/outbox/pallas_call | solution.py:344
  2.0 11.5 %all-to-all-start = ((bf16[128,8,128]{2,1,0:T(8,128)(2,1)}), bf16[128,8,128]{2,1,0:T(8,128)(2,1)S(1)}, u32[]{:S(2)}, u32[]{:S(2)}) async-start(bf16[128,8,128]{2,1,0:T(8,128)(2,1)} %bitcast.12), calls=%async_computation | async-start | bytes 524288 | tf_op jit(solution)/shard_map/all_to_all | solution.py:351
  13.5 5.9 %prepare.1 = (bf16[768,384]{1,0:T(8,128)(2,1)S(1)}, bf16[768,1536]{1,0:T(8,128)(2,1)}, bf16[192,7680]{1,0:T(8,128)(2,1)}, bf16[192,7680]{1,0:T(8,128)(2,1)}, f32[8,384]{1,0:T(8,128)S(1)}) custom-call(bf16[432,384]{1,0:T(8,128)(2,1)} %win_hbm.1, bf16[192,3456]{1,0:T(8,128)(2,1)} %bitcast.11, bf16[192,5184]{1,0:T(8,128)(2,1)} %bitcast.10, f32[384]{0:T(512)} %bin_hbm.1, ...), custom_call_target="tpu_custom_call" | custom-call | flops 10000000 | bytes 16000000 | tf_op jit(solution)/shard_map/prepare/pallas_call | solution.py:354
  19.5 5.5 %all-to-all-done = bf16[128,8,128]{2,1,0:T(8,128)(2,1)S(1)} async-done(((bf16[128,8,128]{2,1,0:T(8,128)(2,1)}), bf16[128,8,128]{2,1,0:T(8,128)(2,1)S(1)}, u32[]{:S(2)}, u32[]{:S(2)}) %all-to-all-start) | async-done | bytes 262176 | tf_op jit(solution)/shard_map/all_to_all | solution.py:351
  25.0 0.6 %route.1 = bf16[512,128]{1,0:T(8,128)(2,1)S(1)} custom-call(bf16[1024,128]{1,0:T(8,128)(2,1)S(1)} %bitcast.7, f32[8,384]{1,0:T(8,128)S(1)} %get-tuple-element.10.after_ref.vec_ref), custom_call_target="tpu_custom_call" | custom-call | tf_op jit(solution)/shard_map/route/pallas_call | solution.py:389
  25.7 8.1 %all_to_all.10 = bf16[8,64,128]{2,1,0:T(8,128)(2,1)S(1)} all-to-all(bf16[8,64,128]{2,1,0:T(8,128)(2,1)S(1)} %bitcast.9), channel_id=1, replica_groups=mesh['seq'=8,'tile'=16] {'seq'}, dimensions={0} | all-to-all | bytes 262144 | tf_op jit(solution)/shard_map/all_to_all | solution.py:397
  33.8 19.9 %decode.1 = bf16[16,8,6144]{2,1,0:T(8,128)(2,1)} custom-call(bf16[512,128]{1,0:T(8,128)(2,1)S(1)} %bitcast.8, bf16[768,384]{1,0:T(8,128)(2,1)S(1)} %get-tuple-element.11.w1_ref, bf16[768,1536]{1,0:T(8,128)(2,1)} %get-tuple-element.12.wc_hbm, bf16[192,7680]{1,0:T(8,128)(2,1)} %get-tuple-element.13.w0_hbm, bf16[192,7680]{1,0:T(8,128)(2,1)} %get-tuple-element.14.wp_hbm, ...), custom_call_target="tpu_custom_call" | custom-call | tf_op jit(solution)/shard_map/decode/pallas_call | solution.py:404
Async XLA Ops:
  2.0 23.0 %all-to-all-start = ((bf16[128,8,128]{2,1,0:T(8,128)(2,1)}), bf16[128,8,128]{2,1,0:T(8,128)(2,1)S(1)}, u32[]{:S(2)}, u32[]{:S(2)}) async-start(bf16[128,8,128]{2,1,0:T(8,128)(2,1)} %bitcast.12), calls=%async_computation | async-start | bytes 524288 | tf_op jit(solution)/shard_map/all_to_all | solution.py:351

commit v5 on v4

--- a/solution.py
+++ b/solution.py
@@ -97,15 +97,25 @@
     b1, g1, bc, g2, b3 = (vec_ref[n : n + 1, :] for n in range(5))
     lane = iota((1, 128), 1)
 
-    i, k = iota((1536, 512), 0), iota((1536, 512), 1)
-    key_i = ((i >> 4) & 31) * 32 + 2 * (i & 7) + ((i >> 3) & 1) - 2 + (i >> 9)
+    i, k = iota((512, 128), 0), iota((1, 512), 1)
+    key_i = (i >> 4) * 32 + 2 * (i & 7) + ((i >> 3) & 1)
     key_k = ((k >> 1) & 31) * 32 + 2 * (k >> 6) + (k & 1)
+    pick = [ones_where(key_i == key_k[:, 128 * n : 128 * n + 128]) for n in range(4)]
     grid_ref[...] = jnp.dot(
-        ones_where(key_i == key_k), recv_ref[...], preferred_element_type=F32
-    ).reshape(3, 8, 4, 16, 128)
+        jnp.concatenate(pick, axis=1), recv_ref[...], preferred_element_type=F32
+    ).reshape(8, 4, 16, 128)
 
     def windows(y, carry):
-        tiles = [[grid_ref[d, y, c] for c in range(4)] for d in range(3)]
+        later = iota((8, 128), 0) > 0
+        tiles = [[], [], []]
+        for c in range(4):
+            now = grid_ref[y, c]
+            even, odd = now[0:8], now[8:16]
+            even_before = jnp.where(later, pltpu.roll(even, 1, 0), 0.0)
+            odd_before = jnp.where(later, pltpu.roll(odd, 1, 0), 0.0)
+            tiles[0].append(jnp.concatenate([even_before, odd_before], axis=0))
+            tiles[1].append(jnp.concatenate([odd_before, even], axis=0))
+            tiles[2].append(now)
         for ix in range(18):
             c, o = divmod((ix + 6) * 16, 128)
 
@@ -129,7 +139,7 @@
         a_ref[iy] = silu(v * scale * g1).astype(BF16).reshape(18, 16, 384)
         return carry
 
-    lax.fori_loop(0, 6, first, 0, unroll=2)
+    lax.fori_loop(0, 6, first, 0, unroll=True)
 
     @pl.when(t == 0)
     def _():
@@ -208,22 +218,28 @@
     def residual(i, carry):
         even, odd = [], []
         for n in range(4):
-            pieces = [[], []]
-            for e in range(3):
-                def tap(shift, low, high):
-                    return jnp.concatenate(
-                        [
-                            r_ref[n, shift, pl.ds(e, 8), i * NI + k, :, low:high].reshape(128, high - low)
-                            for k in range(NI)
-                        ],
-                        axis=0,
-                    )
-
-                pieces[0] += [tap(0, 0, 384), tap(1, 128, 384)]
-                pieces[1] += [tap(0, 0, 256), tap(1, 0, 384)]
-            at = slice(n * 1920, n * 1920 + 1920)
-            even.append(dot_nt(jnp.concatenate(pieces[0], axis=1), w0_ref[:, at]))
-            odd.append(dot_nt(jnp.concatenate(pieces[1], axis=1), wp_ref[:, at]))
+            def tap(shift, e, low, high):
+                return jnp.concatenate(
+                    [
+                        r_ref[n, shift, pl.ds(e, 8), i * NI + k, :, low:high].reshape(128, high - low)
+                        for k in range(NI)
+                    ],
+                    axis=0,
+                )
+
+            def swapped(x):
+                return pltpu.roll(x.astype(F32), 64, 1)
+
+            mids = [[tap(shift, e, 128, 256) for e in range(3)] for shift in range(2)]
+            left_mid = jnp.where(lane < 64, mids[0][0].astype(F32), swapped(mids[0][1])).astype(BF16)
+            right_mid = jnp.where(lane < 64, swapped(mids[1][1]), mids[1][0].astype(F32)).astype(BF16)
+            rights = [tap(1, e, 256, 384) for e in range(3)] + [right_mid, mids[1][2]]
+            lefts = [tap(0, e, 0, 128) for e in range(3)] + [left_mid, mids[0][2]]
+            at = slice(n * 1792, n * 1792 + 1792)
+            even_lhs = jnp.concatenate([tap(0, e, 0, 384) for e in range(3)] + rights, axis=1)
+            odd_lhs = jnp.concatenate([tap(1, e, 0, 384) for e in range(3)] + lefts, axis=1)
+            even.append(dot_nt(even_lhs, w0_ref[:, at]))
+            odd.append(dot_nt(odd_lhs, wp_ref[:, at]))
         slot = i & 1
         for parity in range(2):
             if parity == 0:
@@ -260,7 +276,7 @@
                     at = pl.multiple_of((i * 2 * NI + k) * 384 + c * 128, 128)
                     out_ref[f, :, pl.ds(at, 128)] = rows.astype(BF16)
 
-    wp_ref[0:64, :] = jnp.zeros((64, 7680), BF16)
+    wp_ref[0:64, :] = jnp.zeros((64, 7168), BF16)
     w0_copy.wait()
     wp_copy.wait()
     lax.fori_loop(0, 8 // NI, residual, 0)
@@ -271,19 +287,57 @@
     win_hbm, wup_hbm, wres_hbm, bin_hbm, gin_hbm, bup_hbm, gres_hbm, bres_hbm,
     w1_ref, wc_hbm, w0_hbm, wp_hbm, vec_ref,
     win_ref, wup_ref, wres_ref, bin_ref, gin_ref, bup_ref, gres_ref, bres_ref,
-    wc_ref, w0_ref, wp_ref, sems, out_sems,
+    wc_ref, w0_ref, wp_ref, sems, in_sems, out_sems,
 ):
+    chunks = [pl.ds(48 * n, 48) for n in range(4)]
+    res_in = [
+        pltpu.make_async_copy(wres_hbm.at[at], wres_ref.at[at], in_sems.at[0, n])
+        for n, at in enumerate(chunks)
+    ]
+    up_in = [
+        pltpu.make_async_copy(wup_hbm.at[at], wup_ref.at[at], in_sems.at[1, n])
+        for n, at in enumerate(chunks)
+    ]
     pairs = (
-        (wup_hbm, wup_ref), (wres_hbm, wres_ref), (win_hbm, win_ref), (bin_hbm, bin_ref),
-        (gin_hbm, gin_ref), (bup_hbm, bup_ref), (gres_hbm, gres_ref), (bres_hbm, bres_ref),
+        (win_hbm, win_ref), (bin_hbm, bin_ref), (gin_hbm, gin_ref), (bup_hbm, bup_ref),
+        (gres_hbm, gres_ref), (bres_hbm, bres_ref),
     )
-    copies = [pltpu.make_async_copy(x, y, sems.at[n]) for n, (x, y) in enumerate(pairs)]
-    for copy in copies:
+    rest = [pltpu.make_async_copy(x, y, sems.at[n]) for n, (x, y) in enumerate(pairs)]
+    for copy in res_in + up_in + rest:
         copy.start()
-    copies[0].wait()
+
+    outs = []
+    zero = jnp.zeros((48, 64), BF16)
+    for chunk, rows in enumerate(chunks):
+        res_in[chunk].wait()
+        kinds = [[], [], [], []]
+        for row in range(3):
+            g = [wres_ref[rows, (time * 3 + row) * 576 : (time * 3 + row) * 576 + 576] for time in range(3)]
+            ends = (g[0].astype(F32) + g[2].astype(F32)) * 0.5
+            mid = g[1].astype(F32) * 0.5
+            for kind, tap in zip(kinds, (g[0], (ends + mid).astype(BF16), (ends - mid).astype(BF16), g[2])):
+                kind.append([tap[:, e * 192 : e * 192 + 192] for e in range(3)])
+        for n, w in enumerate(kinds):
+            at = slice(n * 1792, n * 1792 + 1792)
+            even = [w[e][x] for e in range(3) for x in (1, 0)]
+            even += [w[e][2][:, 64:192] for e in range(3)]
+            even += [w[1][2][:, 0:64], w[0][2][:, 0:64], zero, w[2][2][:, 0:64]]
+            odd = [w[e][x] for e in range(3) for x in (2, 1)]
+            odd += [w[e][0][:, 0:128] for e in range(3)]
+            odd += [w[0][0][:, 128:192], w[1][0][:, 128:192], w[2][0][:, 128:192], zero]
+            w0_ref[rows, at] = jnp.concatenate(even, axis=1)
+            wp_ref[rows, at] = jnp.concatenate(odd, axis=1)
+        outs.append(pltpu.make_async_copy(w0_ref.at[rows], w0_hbm.at[rows], out_sems.at[0, chunk]))
+        outs.append(pltpu.make_async_copy(wp_ref.at[rows], wp_hbm.at[rows], out_sems.at[1, chunk]))
+        outs[-2].start()
+        outs[-1].start()
+
     taps = [[[0, 1], [2]], [[0], [1, 2]]]
+    for copy in up_in:
+        copy.wait()
     for dy in range(2):
         for place, dx in enumerate((1, 0)):
+            to = (dy * 2 + place) * 192
             for r in range(2):
                 for c in range(2):
                     total = None
@@ -293,29 +347,12 @@
                             term = wup_ref[:, at : at + 384].astype(F32)
                             total = term if total is None else total + term
                     at = (r * 2 + c) * 384
-                    to = (dy * 2 + place) * 192
                     wc_ref[to : to + 192, at : at + 384] = total.astype(BF16)
-
-    wc_copy = pltpu.make_async_copy(wc_ref, wc_hbm, out_sems.at[0])
-    wc_copy.start()
-    copies[1].wait()
-    zero = jnp.zeros((192, 64), BF16)
-    for row in range(3):
-        g = [wres_ref[:, (time * 3 + row) * 576 : (time * 3 + row) * 576 + 576] for time in range(3)]
-        ends = (g[0].astype(F32) + g[2].astype(F32)) * 0.5
-        mid = g[1].astype(F32) * 0.5
-        taps = (g[0], (ends + mid).astype(BF16), (ends - mid).astype(BF16), g[2])
-        for n, tap in enumerate(taps):
-            w = [tap[:, e * 192 : e * 192 + 192] for e in range(3)]
-            at = slice(n * 1920 + row * 640, n * 1920 + row * 640 + 640)
-            w0_ref[:, at] = jnp.concatenate([w[1], w[0], zero, w[2]], axis=1)
-            wp_ref[:, at] = jnp.concatenate([w[0], zero, w[2], w[1]], axis=1)
-    w0_copy = pltpu.make_async_copy(w0_ref, w0_hbm, out_sems.at[1])
-    wp_copy = pltpu.make_async_copy(wp_ref, wp_hbm, out_sems.at[2])
-    w0_copy.start()
-    wp_copy.start()
-
-    for copy in copies[2:]:
+            rows = pl.ds(to, 192)
+            outs.append(pltpu.make_async_copy(wc_ref.at[rows], wc_hbm.at[rows], out_sems.at[2, dy * 2 + place]))
+            outs[-1].start()
+
+    for copy in rest:
         copy.wait()
     for row in range(3):
         for time in range(3):
@@ -330,9 +367,8 @@
     for row, ref in enumerate((bup_ref, gres_ref, bres_ref)):
         v = ref[...].reshape(1, 192)
         vec_ref[row + 2 : row + 3, :] = jnp.concatenate([v, v], axis=1)
-    wc_copy.wait()
-    w0_copy.wait()
-    wp_copy.wait()
+    for copy in outs:
+        copy.wait()
 
 
 VMEM_SPEC = pl.BlockSpec(memory_space=pltpu.VMEM)
@@ -356,8 +392,8 @@
         out_shape=[
             jax.ShapeDtypeStruct((768, 384), BF16),
             pltpu.HBM((768, 1536), BF16),
-            pltpu.HBM((192, 7680), BF16),
-            pltpu.HBM((192, 7680), BF16),
+            pltpu.HBM((192, 7168), BF16),
+            pltpu.HBM((192, 7168), BF16),
             jax.ShapeDtypeStruct((8, 384), F32),
         ],
         in_specs=[HBM_SPEC] * 8,
@@ -372,10 +408,11 @@
             pltpu.VMEM((192,), F32),
             pltpu.VMEM((192,), F32),
             pltpu.VMEM((768, 1536), BF16),
-            pltpu.VMEM((192, 7680), BF16),
-            pltpu.VMEM((192, 7680), BF16),
-            pltpu.SemaphoreType.DMA((8,)),
-            pltpu.SemaphoreType.DMA((3,)),
+            pltpu.VMEM((192, 7168), BF16),
+            pltpu.VMEM((192, 7168), BF16),
+            pltpu.SemaphoreType.DMA((6,)),
+            pltpu.SemaphoreType.DMA((2, 4)),
+            pltpu.SemaphoreType.DMA((3, 4)),
         ],
         cost_estimate=pl.CostEstimate(flops=10_000_000, bytes_accessed=16_000_000, transcendentals=0),
         compiler_params=pltpu.CompilerParams(vmem_limit_bytes=28 * 1024 * 1024),
@@ -407,15 +444,15 @@
         in_specs=[VMEM_SPEC] * 2 + [HBM_SPEC] * 3 + [VMEM_SPEC],
         out_specs=VMEM_SPEC,
         scratch_shapes=[
-            pltpu.VMEM((3, 8, 4, 16, 128), F32),
+            pltpu.VMEM((8, 4, 16, 128), F32),
             pltpu.VMEM((8, 18, 16, 256), BF16),
             pltpu.VMEM((6, 18, 16, 384), BF16),
             pltpu.VMEM((10, 17, 16, 384), BF16),
             pltpu.VMEM((4, 2, 10, 8, 16, 384), BF16),
             pltpu.VMEM((2, 2 * NI, 2, 3, 64, 128), F32),
             pltpu.VMEM((768, 1536), BF16),
-            pltpu.VMEM((192, 7680), BF16),
-            pltpu.VMEM((256, 7680), BF16),
+            pltpu.VMEM((192, 7168), BF16),
+            pltpu.VMEM((256, 7168), BF16),
             pltpu.SemaphoreType.DMA((3,)),
         ],
         compiler_params=pltpu.CompilerParams(vmem_limit_bytes=44 * 1024 * 1024),

time: 54.1 us -> 52.5 us (0.970)
  Pallas kernels: 28.5 us -> 25.7 us
  waiting for transfers between devices: 5.53 us -> 6.73 us
    pallas_call x1, Pallas kernels: 19.9 us -> 18.3 us  [decode(): pl.pallas_call(decode_kernel, out_shape=jax.ShapeDtypeStruct((16, 8, 6144...]
    all_to_all x1, waiting for transfers between devices: 5.53 us -> 6.73 us  [local(): lax.all_to_all(outbox.reshape(128, 8, 128), ('seq', 'tile'), split_axis=0...]
    pallas_call x1, Pallas kernels: 5.93 us -> 4.73 us  [local(): pl.pallas_call(prepare_kernel, out_shape=[jax.ShapeDtypeStruct((768, 384)...]
  transfers between devices with their start and end apart: 1 -> 1, of which waited for: 1 -> 1; matrix products, arithmetic and copies ran while one was open for 0% -> 0% of each run, Pallas kernels for 11% -> 9%
where the time goes in v5:
time: 52.5 us; the launch traced here: 52.3 us
  Pallas kernels  25.7 us (49%)
  starting transfers between devices  11.5 us (22%)
  blocking collectives  8.14 us (16%)
  waiting for transfers between devices  6.73 us (13%)
    pallas_call x1, Pallas kernels, decode(): pl.pallas_call(decode_kernel, out_shape=jax.ShapeDtypeStruct((16, 8, 6144...  18.3 us
    all_to_all x1, starting transfers between devices, local(): lax.all_to_all(outbox.reshape(128, 8, 128), ('seq', 'tile'), split_axis=0...  11.5 us
    all_to_all x1, blocking collectives, local(): lax.all_to_all(routed.reshape(8, 64, 128), 'seq', split_axis=0, concat_ax...  8.14 us
    all_to_all x1, waiting for transfers between devices, local(): lax.all_to_all(outbox.reshape(128, 8, 128), ('seq', 'tile'), split_axis=0...  6.73 us
    pallas_call x1, Pallas kernels, local(): pl.pallas_call(prepare_kernel, out_shape=[jax.ShapeDtypeStruct((768, 384)...  4.73 us
    pallas_call x1, Pallas kernels, local(): pl.pallas_call(outbox_kernel, out_shape=jax.ShapeDtypeStruct((1024, 128),...  2.04 us
  transfers between devices with their start and end apart: 1, of which 1 were waited for; matrix products, arithmetic and copies ran while one was open for 0% of the time, Pallas kernels for 9%

profile of v5, /device:TPU:1, one launch (start us, length us, event | category | flops | bytes accessed | tf_op | source)
XLA Modules:
  0.0 52.3 jit_solution(10906389445003742898)
XLA Ops:
  0.0 2.0 %outbox.1 = bf16[1024,128]{1,0:T(8,128)(2,1)} custom-call(s32[1,128]{1,0:T(1,128)} %bitcast.13, bf16[128,128]{1,0:T(8,128)(2,1)} %lat_ref.1), custom_call_target="tpu_custom_call" | custom-call | tf_op jit(solution)/shard_map/outbox/pallas_call | solution.py:380
  2.0 11.5 %all-to-all-start = ((bf16[128,8,128]{2,1,0:T(8,128)(2,1)}), bf16[128,8,128]{2,1,0:T(8,128)(2,1)S(1)}, u32[]{:S(2)}, u32[]{:S(2)}) async-start(bf16[128,8,128]{2,1,0:T(8,128)(2,1)} %bitcast.12), calls=%async_computation | async-start | bytes 524288 | tf_op jit(solution)/shard_map/all_to_all | solution.py:387
  13.5 4.7 %prepare.1 = (bf16[768,384]{1,0:T(8,128)(2,1)S(1)}, bf16[768,1536]{1,0:T(8,128)(2,1)}, bf16[192,7168]{1,0:T(8,128)(2,1)}, bf16[192,7168]{1,0:T(8,128)(2,1)}, f32[8,384]{1,0:T(8,128)S(1)}) custom-call(bf16[432,384]{1,0:T(8,128)(2,1)} %win_hbm.1, bf16[192,3456]{1,0:T(8,128)(2,1)} %bitcast.11, bf16[192,5184]{1,0:T(8,128)(2,1)} %bitcast.10, f32[384]{0:T(512)} %bin_hbm.1, ...), custom_call_target="tpu_custom_call" | custom-call | flops 10000000 | bytes 16000000 | tf_op jit(solution)/shard_map/prepare/pallas_call | solution.py:390
  18.3 6.7 %all-to-all-done = bf16[128,8,128]{2,1,0:T(8,128)(2,1)S(1)} async-done(((bf16[128,8,128]{2,1,0:T(8,128)(2,1)}), bf16[128,8,128]{2,1,0:T(8,128)(2,1)S(1)}, u32[]{:S(2)}, u32[]{:S(2)}) %all-to-all-start) | async-done | bytes 262176 | tf_op jit(solution)/shard_map/all_to_all | solution.py:387
  25.0 0.6 %route.1 = bf16[512,128]{1,0:T(8,128)(2,1)S(1)} custom-call(bf16[1024,128]{1,0:T(8,128)(2,1)S(1)} %bitcast.7, f32[8,384]{1,0:T(8,128)S(1)} %get-tuple-element.10.after_ref.vec_ref), custom_call_target="tpu_custom_call" | custom-call | tf_op jit(solution)/shard_map/route/pallas_call | solution.py:426
  25.7 8.1 %all_to_all.10 = bf16[8,64,128]{2,1,0:T(8,128)(2,1)S(1)} all-to-all(bf16[8,64,128]{2,1,0:T(8,128)(2,1)S(1)} %bitcast.9), channel_id=1, replica_groups=mesh['seq'=8,'tile'=16] {'seq'}, dimensions={0} | all-to-all | bytes 262144 | tf_op jit(solution)/shard_map/all_to_all | solution.py:434
  33.8 18.3 %decode.1 = bf16[16,8,6144]{2,1,0:T(8,128)(2,1)} custom-call(bf16[512,128]{1,0:T(8,128)(2,1)S(1)} %bitcast.8, bf16[768,384]{1,0:T(8,128)(2,1)S(1)} %get-tuple-element.11.w1_ref, bf16[768,1536]{1,0:T(8,128)(2,1)} %get-tuple-element.12.wc_hbm, bf16[192,7168]{1,0:T(8,128)(2,1)} %get-tuple-element.13.w0_hbm, bf16[192,7168]{1,0:T(8,128)(2,1)} %get-tuple-element.14.wp_hbm, ...), custom_call_target="tpu_custom_call" | custom-call | tf_op jit(solution)/shard_map/decode/pallas_call | solution.py:441
Async XLA Ops:
  2.0 23.0 %all-to-all-start = ((bf16[128,8,128]{2,1,0:T(8,128)(2,1)}), bf16[128,8,128]{2,1,0:T(8,128)(2,1)S(1)}, u32[]{:S(2)}, u32[]{:S(2)}) async-start(bf16[128,8,128]{2,1,0:T(8,128)(2,1)} %bitcast.12), calls=%async_computation | async-start | bytes 524288 | tf_op jit(solution)/shard_map/all_to_all | solution.py:387

commit v6 on v5

--- a/solution.py
+++ b/solution.py
@@ -105,7 +105,7 @@
         jnp.concatenate(pick, axis=1), recv_ref[...], preferred_element_type=F32
     ).reshape(8, 4, 16, 128)
 
-    def windows(y, carry):
+    def windows(y):
         later = iota((8, 128), 0) > 0
         tiles = [[], [], []]
         for c in range(4):
@@ -128,41 +128,37 @@
 
             x_ref[y, ix, :, 0:128] = jnp.where(lane < 64, window(0, 0), window(1, 64)).astype(BF16)
             x_ref[y, ix, :, 128:256] = window(2, 0).astype(BF16)
-        return carry
-
-    lax.fori_loop(0, 8, windows, 0)
-
-    def first(iy, carry):
+
+    for y in range(8):
+        windows(y)
+
+    def inside(condition):
+        return jnp.where(condition, 1.0, 0.0)
+
+    has_low_row, has_high_row = inside(t > 0), inside(t < lax.axis_size("tile") - 1)
+    has_low_col, has_high_col = inside(s > 0), inside(s < lax.axis_size("seq") - 1)
+
+    def first(iy):
         lhs = jnp.concatenate([x_ref[iy + d].reshape(288, 256) for d in range(3)], axis=1)
         v = jnp.dot(lhs, w1_ref[...], preferred_element_type=F32) + b1
         scale = lax.rsqrt(jnp.mean(v * v, axis=1, keepdims=True) + 1e-06)
+        row = iota((288, 1), 0)
+        scale = jnp.where(row < 16, scale * has_low_col, scale)
+        scale = jnp.where(row >= 272, scale * has_high_col, scale)
+        if iy == 0:
+            scale = scale * has_low_row
+        if iy == 5:
+            scale = scale * has_high_row
         a_ref[iy] = silu(v * scale * g1).astype(BF16).reshape(18, 16, 384)
-        return carry
-
-    lax.fori_loop(0, 6, first, 0, unroll=True)
-
-    @pl.when(t == 0)
-    def _():
-        a_ref[0] = jnp.zeros((18, 16, 384), BF16)
-
-    @pl.when(t == lax.axis_size("tile") - 1)
-    def _():
-        a_ref[5] = jnp.zeros((18, 16, 384), BF16)
-
-    @pl.when(s == 0)
-    def _():
-        a_ref[:, 0] = jnp.zeros((6, 16, 384), BF16)
-
-    @pl.when(s == lax.axis_size("seq") - 1)
-    def _():
-        a_ref[:, 17] = jnp.zeros((6, 16, 384), BF16)
-
+
+    for iy in range(6):
+        first(iy)
 
     wc_copy.wait()
 
-    def corners(ci, carry):
+    def corners(ci):
         lhs = jnp.concatenate(
-            [a_ref[ci + d, pl.ds(e, 17)].reshape(272, 384) for d in range(2) for e in range(2)],
+            [a_ref[ci + d, e : e + 17].reshape(272, 384) for d in range(2) for e in range(2)],
             axis=1,
         )
         acc = dot_nt(lhs, wc_ref[...])
@@ -176,6 +172,13 @@
             top = jnp.sum(sq[:, 256:384] + jnp.where(lane < 64, 0.0, mid), axis=1, keepdims=True)
             low = lax.rsqrt(low * (1 / 192) + 1e-06)
             top = lax.rsqrt(top * (1 / 192) + 1e-06)
+            row = iota((272, 1), 0)
+            low = jnp.where(row >= 256, low * has_high_col, low)
+            top = jnp.where(row < 16, top * has_low_col, top)
+            if 2 * ci + d == 0:
+                low, top = low * has_low_row, top * has_low_row
+            if 2 * ci + d == 9:
+                low, top = low * has_high_row, top * has_high_row
             low = jnp.broadcast_to(low, (272, 128))
             top = jnp.broadcast_to(top, (272, 128))
             scale = jnp.concatenate([low, jnp.where(lane < 64, low, top), top], axis=1)
@@ -187,33 +190,9 @@
             for n, v in enumerate((d0 - d2, d1 + d2, d2 - d1, d1 - d3)):
                 r_ref[n, 0, 2 * ci + d] = v[0:16].reshape(8, 16, 384).astype(BF16)
                 r_ref[n, 1, 2 * ci + d] = v[1:17].reshape(8, 16, 384).astype(BF16)
-        return carry
-
-    lax.fori_loop(0, 5, corners, 0, unroll=True)
-
-    @pl.when(t == 0)
-    def _():
-        for n in range(4):
-            r_ref[n, :, 0] = jnp.zeros((2, 8, 16, 384), BF16)
-
-    @pl.when(t == lax.axis_size("tile") - 1)
-    def _():
-        for n in range(4):
-            r_ref[n, :, 9] = jnp.zeros((2, 8, 16, 384), BF16)
-
-    row, wide = iota((1, 16, 384), 1), iota((1, 16, 384), 2)
-
-    @pl.when(s == 0)
-    def _():
-        for n in range(4):
-            v = r_ref[n, 0, :, 0].astype(F32)
-            r_ref[n, 0, :, 0] = jnp.where((wide < 192) | (row >= 8), v, 0.0).astype(BF16)
-
-    @pl.when(s == lax.axis_size("seq") - 1)
-    def _():
-        for n in range(4):
-            v = r_ref[n, 1, :, 7].astype(F32)
-            r_ref[n, 1, :, 7] = jnp.where((wide >= 192) | (row < 8), v, 0.0).astype(BF16)
+
+    for ci in range(5):
+        corners(ci)
 
     def residual(i, carry):
         even, odd = [], []

time: 52.5 us -> 51.4 us (0.979)
  Pallas kernels: 25.7 us -> 24.6 us
    pallas_call x1, Pallas kernels: 18.3 us -> 17.2 us  [decode(): pl.pallas_call(decode_kernel, out_shape=jax.ShapeDtypeStruct((16, 8, 6144...]
where the time goes in v6:
time: 51.4 us; the launch traced here: 51.1 us
  Pallas kernels  24.6 us (48%)
  starting transfers between devices  11.5 us (22%)
  blocking collectives  8.14 us (16%)
  waiting for transfers between devices  6.73 us (13%)
    pallas_call x1, Pallas kernels, decode(): pl.pallas_call(decode_kernel, out_shape=jax.ShapeDtypeStruct((16, 8, 6144...  17.2 us
    all_to_all x1, starting transfers between devices, local(): lax.all_to_all(outbox.reshape(128, 8, 128), ('seq', 'tile'), split_axis=0...  11.5 us
    all_to_all x1, blocking collectives, local(): lax.all_to_all(routed.reshape(8, 64, 128), 'seq', split_axis=0, concat_ax...  8.14 us
    all_to_all x1, waiting for transfers between devices, local(): lax.all_to_all(outbox.reshape(128, 8, 128), ('seq', 'tile'), split_axis=0...  6.73 us
    pallas_call x1, Pallas kernels, local(): pl.pallas_call(prepare_kernel, out_shape=[jax.ShapeDtypeStruct((768, 384)...  4.73 us
    pallas_call x1, Pallas kernels, local(): pl.pallas_call(outbox_kernel, out_shape=jax.ShapeDtypeStruct((1024, 128),...  2.04 us
  transfers between devices with their start and end apart: 1, of which 1 were waited for; matrix products, arithmetic and copies ran while one was open for 0% of the time, Pallas kernels for 9%

profile of v6, /device:TPU:1, one launch (start us, length us, event | category | flops | bytes accessed | tf_op | source)
XLA Modules:
  0.0 51.1 jit_solution(9077192660782176042)
XLA Ops:
  0.0 2.0 %outbox.1 = bf16[1024,128]{1,0:T(8,128)(2,1)} custom-call(s32[1,128]{1,0:T(1,128)} %bitcast.13, bf16[128,128]{1,0:T(8,128)(2,1)} %lat_ref.1), custom_call_target="tpu_custom_call" | custom-call | tf_op jit(solution)/shard_map/outbox/pallas_call | solution.py:359
  2.0 11.5 %all-to-all-start = ((bf16[128,8,128]{2,1,0:T(8,128)(2,1)}), bf16[128,8,128]{2,1,0:T(8,128)(2,1)S(1)}, u32[]{:S(2)}, u32[]{:S(2)}) async-start(bf16[128,8,128]{2,1,0:T(8,128)(2,1)} %bitcast.12), calls=%async_computation | async-start | bytes 524288 | tf_op jit(solution)/shard_map/all_to_all | solution.py:366
  13.5 4.7 %prepare.1 = (bf16[768,384]{1,0:T(8,128)(2,1)S(1)}, bf16[768,1536]{1,0:T(8,128)(2,1)}, bf16[192,7168]{1,0:T(8,128)(2,1)}, bf16[192,7168]{1,0:T(8,128)(2,1)}, f32[8,384]{1,0:T(8,128)S(1)}) custom-call(bf16[432,384]{1,0:T(8,128)(2,1)} %win_hbm.1, bf16[192,3456]{1,0:T(8,128)(2,1)} %bitcast.11, bf16[192,5184]{1,0:T(8,128)(2,1)} %bitcast.10, f32[384]{0:T(512)} %bin_hbm.1, ...), custom_call_target="tpu_custom_call" | custom-call | flops 10000000 | bytes 16000000 | tf_op jit(solution)/shard_map/prepare/pallas_call | solution.py:369
  18.3 6.7 %all-to-all-done = bf16[128,8,128]{2,1,0:T(8,128)(2,1)S(1)} async-done(((bf16[128,8,128]{2,1,0:T(8,128)(2,1)}), bf16[128,8,128]{2,1,0:T(8,128)(2,1)S(1)}, u32[]{:S(2)}, u32[]{:S(2)}) %all-to-all-start) | async-done | bytes 262176 | tf_op jit(solution)/shard_map/all_to_all | solution.py:366
  25.0 0.6 %route.1 = bf16[512,128]{1,0:T(8,128)(2,1)S(1)} custom-call(bf16[1024,128]{1,0:T(8,128)(2,1)S(1)} %bitcast.7, f32[8,384]{1,0:T(8,128)S(1)} %get-tuple-element.10.after_ref.vec_ref), custom_call_target="tpu_custom_call" | custom-call | tf_op jit(solution)/shard_map/route/pallas_call | solution.py:405
  25.7 8.1 %all_to_all.10 = bf16[8,64,128]{2,1,0:T(8,128)(2,1)S(1)} all-to-all(bf16[8,64,128]{2,1,0:T(8,128)(2,1)S(1)} %bitcast.9), channel_id=1, replica_groups=mesh['seq'=8,'tile'=16] {'seq'}, dimensions={0} | all-to-all | bytes 262144 | tf_op jit(solution)/shard_map/all_to_all | solution.py:413
  33.8 17.2 %decode.1 = bf16[16,8,6144]{2,1,0:T(8,128)(2,1)} custom-call(bf16[512,128]{1,0:T(8,128)(2,1)S(1)} %bitcast.8, bf16[768,384]{1,0:T(8,128)(2,1)S(1)} %get-tuple-element.11.w1_ref, bf16[768,1536]{1,0:T(8,128)(2,1)} %get-tuple-element.12.wc_hbm, bf16[192,7168]{1,0:T(8,128)(2,1)} %get-tuple-element.13.w0_hbm, bf16[192,7168]{1,0:T(8,128)(2,1)} %get-tuple-element.14.wp_hbm, ...), custom_call_target="tpu_custom_call" | custom-call | tf_op jit(solution)/shard_map/decode/pallas_call | solution.py:420
Async XLA Ops:
  2.0 23.0 %all-to-all-start = ((bf16[128,8,128]{2,1,0:T(8,128)(2,1)}), bf16[128,8,128]{2,1,0:T(8,128)(2,1)S(1)}, u32[]{:S(2)}, u32[]{:S(2)}) async-start(bf16[128,8,128]{2,1,0:T(8,128)(2,1)} %bitcast.12), calls=%async_computation | async-start | bytes 524288 | tf_op jit(solution)/shard_map/all_to_all | solution.py:366

commit v7 on v6

--- a/solution.py
+++ b/solution.py
@@ -64,13 +64,17 @@
     slot, lane = iota(boxes.shape, 1), iota(boxes.shape, 2)
     label = jnp.sum(jnp.where((slot == lane) & (slot < 6), labels, 0.0), axis=2, keepdims=True)
     label = label.reshape(rows, 1).astype(I32)
+    lane = iota((1, 128), 1)
     k = iota((1, 512), 1)
-    group = 2 * (k >> 6) - 1 + ((k >> 1) & 3)
-    wanted = ((k & 1) * 8 + ((k >> 3) & 7)) * 16 + group + 1
+    group = 2 * (k >> 6) - 1 + ((k >> 4) & 3)
+    wanted = ((k & 1) * 8 + ((k >> 1) & 7)) * 16 + group + 1
     wanted = jnp.where((group >= 0) & (group < 16), wanted, -1)
     pick = ones_where(label == wanted)
-    out = lax.dot_general(pick, inbox, (((0,), (0,)), ((), ())), preferred_element_type=F32)
-    out_ref[...] = out.astype(BF16)
+    got = lax.dot_general(pick, inbox, (((0,), (0,)), ((), ())), preferred_element_type=F32)
+    for target in range(8):
+        rows = got[64 * target : 64 * target + 64]
+        halo = jnp.where(lane < 64, rows[48:64], rows[0:16])
+        out_ref[48 * target : 48 * target + 48] = jnp.concatenate([rows[16:48], halo], axis=0).astype(BF16)
 
 
 def dot_nt(x, w):
@@ -83,8 +87,8 @@
 
 
 def decode_kernel(
-    recv_ref, w1_ref, wc_hbm, w0_hbm, wp_hbm, vec_ref, out_ref,
-    grid_ref, x_ref, a_ref, u_ref, r_ref, fin_ref, wc_ref, w0_ref, wp_ref, sems,
+    recv_ref, w1_ref, wc_hbm, w0_hbm, wp_hbm, vec_ref, out_hbm,
+    grid_ref, x_ref, a_ref, u_ref, r_ref, fin_ref, wc_ref, w0_ref, wp_ref, out_ref, sems, out_sems,
 ):
     s = lax.axis_index("seq")
     t = lax.axis_index("tile")
@@ -97,25 +101,28 @@
     b1, g1, bc, g2, b3 = (vec_ref[n : n + 1, :] for n in range(5))
     lane = iota((1, 128), 1)
 
-    i, k = iota((512, 128), 0), iota((1, 512), 1)
+    i, k = iota((384, 128), 0), iota((1, 384), 1)
+    source = k // 48
     key_i = (i >> 4) * 32 + 2 * (i & 7) + ((i >> 3) & 1)
-    key_k = ((k >> 1) & 31) * 32 + 2 * (k >> 6) + (k & 1)
-    pick = [ones_where(key_i == key_k[:, 128 * n : 128 * n + 128]) for n in range(4)]
+    key_k = ((k - 48 * source) >> 1) * 32 + 2 * source + (k & 1)
+    pick = [ones_where(key_i == key_k[:, 128 * n : 128 * n + 128]) for n in range(3)]
     grid_ref[...] = jnp.dot(
         jnp.concatenate(pick, axis=1), recv_ref[...], preferred_element_type=F32
-    ).reshape(8, 4, 16, 128)
+    ).reshape(3, 8, 16, 128)
 
     def windows(y):
         later = iota((8, 128), 0) > 0
         tiles = [[], [], []]
-        for c in range(4):
-            now = grid_ref[y, c]
+        for c in (2, 0, 1):
+            now = grid_ref[c, y]
             even, odd = now[0:8], now[8:16]
             even_before = jnp.where(later, pltpu.roll(even, 1, 0), 0.0)
             odd_before = jnp.where(later, pltpu.roll(odd, 1, 0), 0.0)
             tiles[0].append(jnp.concatenate([even_before, odd_before], axis=0))
             tiles[1].append(jnp.concatenate([odd_before, even], axis=0))
             tiles[2].append(now)
+        for group in tiles:
+            group.append(group[0])
         for ix in range(18):
             c, o = divmod((ix + 6) * 16, 128)
 
@@ -219,7 +226,6 @@
             odd_lhs = jnp.concatenate([tap(1, e, 0, 384) for e in range(3)] + lefts, axis=1)
             even.append(dot_nt(even_lhs, w0_ref[:, at]))
             odd.append(dot_nt(odd_lhs, wp_ref[:, at]))
-        slot = i & 1
         for parity in range(2):
             if parity == 0:
                 p, q = (v[0] + (v[1] + v[2]) for v in (even, odd))
@@ -242,24 +248,24 @@
                         qk[..., 128:256] + b3[:, 256:384] + right[..., 256:384],
                     )
                     for z, part in enumerate(parts):
-                        fin_ref[slot, 2 * k + c, parity, z] = part.reshape(64, 128)
-        finish(i - 1, 1 - slot)
+                        fin_ref[m, parity, z] = part.reshape(64, 128)
         return carry
-
-    def finish(i, slot):
-        i = jnp.maximum(i, 0)
-        for k in range(2 * NI):
-            for c in range(3):
-                for f in range(16):
-                    rows = fin_ref[slot, k, f & 1, c, pl.ds(f >> 1, 8, stride=8), :]
-                    at = pl.multiple_of((i * 2 * NI + k) * 384 + c * 128, 128)
-                    out_ref[f, :, pl.ds(at, 128)] = rows.astype(BF16)
 
     wp_ref[0:64, :] = jnp.zeros((64, 7168), BF16)
     w0_copy.wait()
     wp_copy.wait()
-    lax.fori_loop(0, 8 // NI, residual, 0)
-    finish(8 // NI - 1, (8 // NI - 1) & 1)
+    for i in range(8 // NI):
+        residual(i, 0)
+    outs = []
+    for f in range(16):
+        for m in range(16):
+            for c in range(3):
+                rows = fin_ref[m, f & 1, c, pl.ds(f >> 1, 8, stride=8), :]
+                out_ref[f, :, 384 * m + 128 * c : 384 * m + 128 * c + 128] = rows.astype(BF16)
+        outs.append(pltpu.make_async_copy(out_ref.at[f], out_hbm.at[f], out_sems.at[f]))
+        outs[-1].start()
+    for copy in outs:
+        copy.wait()
 
 
 def prepare_kernel(
@@ -404,15 +410,15 @@
     )
     routed = pl.pallas_call(
         route_kernel,
-        out_shape=jax.ShapeDtypeStruct((512, 128), BF16),
+        out_shape=jax.ShapeDtypeStruct((384, 128), BF16),
         in_specs=[VMEM_SPEC, ANY_SPEC],
         out_specs=VMEM_SPEC,
         compiler_params=pltpu.CompilerParams(vmem_limit_bytes=12 * 1024 * 1024),
         name="route",
     )(inbox.reshape(1024, 128), prepared[4])
     recv = lax.all_to_all(
-        routed.reshape(8, 64, 128), "seq", split_axis=0, concat_axis=0, tiled=True
-    ).reshape(512, 128)
+        routed.reshape(8, 48, 128), "seq", split_axis=0, concat_axis=0, tiled=True
+    ).reshape(384, 128)
     return decode(recv, *prepared)
 
 
@@ -421,18 +427,20 @@
         decode_kernel,
         out_shape=jax.ShapeDtypeStruct((16, 8, 6144), BF16),
         in_specs=[VMEM_SPEC] * 2 + [HBM_SPEC] * 3 + [VMEM_SPEC],
-        out_specs=VMEM_SPEC,
+        out_specs=HBM_SPEC,
         scratch_shapes=[
-            pltpu.VMEM((8, 4, 16, 128), F32),
+            pltpu.VMEM((3, 8, 16, 128), F32),
             pltpu.VMEM((8, 18, 16, 256), BF16),
             pltpu.VMEM((6, 18, 16, 384), BF16),
             pltpu.VMEM((10, 17, 16, 384), BF16),
             pltpu.VMEM((4, 2, 10, 8, 16, 384), BF16),
-            pltpu.VMEM((2, 2 * NI, 2, 3, 64, 128), F32),
+            pltpu.VMEM((16, 2, 3, 64, 128), F32),
             pltpu.VMEM((768, 1536), BF16),
             pltpu.VMEM((192, 7168), BF16),
             pltpu.VMEM((256, 7168), BF16),
+            pltpu.VMEM((16, 8, 6144), BF16),
             pltpu.SemaphoreType.DMA((3,)),
+            pltpu.SemaphoreType.DMA((16,)),
         ],
         compiler_params=pltpu.CompilerParams(vmem_limit_bytes=44 * 1024 * 1024),
         name="decode",

time: 51.4 us -> 50.7 us (0.986)
  no operation moved by 1% of the time
where the time goes in v7:
time: 50.7 us; the launch traced here: 50.5 us
  Pallas kernels  24.2 us (48%)
  starting transfers between devices  11.5 us (23%)
  blocking collectives  7.84 us (15%)
  waiting for transfers between devices  6.73 us (13%)
    pallas_call x1, Pallas kernels, decode(): pl.pallas_call(decode_kernel, out_shape=jax.ShapeDtypeStruct((16, 8, 6144...  16.8 us
    all_to_all x1, starting transfers between devices, local(): lax.all_to_all(outbox.reshape(128, 8, 128), ('seq', 'tile'), split_axis=0...  11.5 us
    all_to_all x1, blocking collectives, local(): lax.all_to_all(routed.reshape(8, 48, 128), 'seq', split_axis=0, concat_ax...  7.84 us
    all_to_all x1, waiting for transfers between devices, local(): lax.all_to_all(outbox.reshape(128, 8, 128), ('seq', 'tile'), split_axis=0...  6.73 us
    pallas_call x1, Pallas kernels, local(): pl.pallas_call(prepare_kernel, out_shape=[jax.ShapeDtypeStruct((768, 384)...  4.73 us
    pallas_call x1, Pallas kernels, local(): pl.pallas_call(outbox_kernel, out_shape=jax.ShapeDtypeStruct((1024, 128),...  2.04 us
  transfers between devices with their start and end apart: 1, of which 1 were waited for; matrix products, arithmetic and copies ran while one was open for 0% of the time, Pallas kernels for 9%

profile of v7, /device:TPU:1, one launch (start us, length us, event | category | flops | bytes accessed | tf_op | source)
XLA Modules:
  0.0 50.5 jit_solution(16370723765734936744)
XLA Ops:
  0.0 2.0 %outbox.1 = bf16[1024,128]{1,0:T(8,128)(2,1)} custom-call(s32[1,128]{1,0:T(1,128)} %bitcast.13, bf16[128,128]{1,0:T(8,128)(2,1)} %lat_ref.1), custom_call_target="tpu_custom_call" | custom-call | tf_op jit(solution)/shard_map/outbox/pallas_call | solution.py:365
  2.0 11.5 %all-to-all-start = ((bf16[128,8,128]{2,1,0:T(8,128)(2,1)}), bf16[128,8,128]{2,1,0:T(8,128)(2,1)S(1)}, u32[]{:S(2)}, u32[]{:S(2)}) async-start(bf16[128,8,128]{2,1,0:T(8,128)(2,1)} %bitcast.12), calls=%async_computation | async-start | bytes 524288 | tf_op jit(solution)/shard_map/all_to_all | solution.py:372
  13.5 4.7 %prepare.1 = (bf16[768,384]{1,0:T(8,128)(2,1)S(1)}, bf16[768,1536]{1,0:T(8,128)(2,1)}, bf16[192,7168]{1,0:T(8,128)(2,1)}, bf16[192,7168]{1,0:T(8,128)(2,1)}, f32[8,384]{1,0:T(8,128)S(1)}) custom-call(bf16[432,384]{1,0:T(8,128)(2,1)} %win_hbm.1, bf16[192,3456]{1,0:T(8,128)(2,1)} %bitcast.11, bf16[192,5184]{1,0:T(8,128)(2,1)} %bitcast.10, f32[384]{0:T(512)} %bin_hbm.1, ...), custom_call_target="tpu_custom_call" | custom-call | flops 10000000 | bytes 16000000 | tf_op jit(solution)/shard_map/prepare/pallas_call | solution.py:375
  18.3 6.7 %all-to-all-done = bf16[128,8,128]{2,1,0:T(8,128)(2,1)S(1)} async-done(((bf16[128,8,128]{2,1,0:T(8,128)(2,1)}), bf16[128,8,128]{2,1,0:T(8,128)(2,1)S(1)}, u32[]{:S(2)}, u32[]{:S(2)}) %all-to-all-start) | async-done | bytes 262176 | tf_op jit(solution)/shard_map/all_to_all | solution.py:372
  25.0 0.6 %route.1 = bf16[384,128]{1,0:T(8,128)(2,1)S(1)} custom-call(bf16[1024,128]{1,0:T(8,128)(2,1)S(1)} %bitcast.7, f32[8,384]{1,0:T(8,128)S(1)} %get-tuple-element.10.after_ref.vec_ref), custom_call_target="tpu_custom_call" | custom-call | tf_op jit(solution)/shard_map/route/pallas_call | solution.py:411
  25.7 7.8 %all_to_all.10 = bf16[8,48,128]{2,1,0:T(8,128)(2,1)S(1)} all-to-all(bf16[8,48,128]{2,1,0:T(8,128)(2,1)S(1)} %bitcast.9), channel_id=1, replica_groups=mesh['seq'=8,'tile'=16] {'seq'}, dimensions={0} | all-to-all | bytes 196608 | tf_op jit(solution)/shard_map/all_to_all | solution.py:419
  33.5 16.8 %decode.1 = bf16[16,8,6144]{2,1,0:T(8,128)(2,1)} custom-call(bf16[384,128]{1,0:T(8,128)(2,1)S(1)} %bitcast.8, bf16[768,384]{1,0:T(8,128)(2,1)S(1)} %get-tuple-element.11.w1_ref, bf16[768,1536]{1,0:T(8,128)(2,1)} %get-tuple-element.12.wc_hbm, bf16[192,7168]{1,0:T(8,128)(2,1)} %get-tuple-element.13.w0_hbm, bf16[192,7168]{1,0:T(8,128)(2,1)} %get-tuple-element.14.wp_hbm, ...), custom_call_target="tpu_custom_call" | custom-call | tf_op jit(solution)/shard_map/decode/pallas_call | solution.py:426
Async XLA Ops:
  2.0 23.0 %all-to-all-start = ((bf16[128,8,128]{2,1,0:T(8,128)(2,1)}), bf16[128,8,128]{2,1,0:T(8,128)(2,1)S(1)}, u32[]{:S(2)}, u32[]{:S(2)}) async-start(bf16[128,8,128]{2,1,0:T(8,128)(2,1)} %bitcast.12), calls=%async_computation | async-start | bytes 524288 | tf_op jit(solution)/shard_map/all_to_all | solution.py:372

commit v8 on v7

--- a/solution.py
+++ b/solution.py
@@ -19,7 +19,9 @@
     return jnp.where(cond, 1.0, 0.0).astype(BF16)
 
 
-def outbox_kernel(slot_ref, lat_ref, out_ref):
+def outbox_kernel(slot_ref, lat_hbm, out_hbm, lat_ref, out_ref, sem, out_sems):
+    fetch = pltpu.make_async_copy(lat_hbm, lat_ref, sem)
+    fetch.start()
     n = 128
     row = jnp.broadcast_to(slot_ref[...], (n, n))
     col = jnp.transpose(row)
@@ -46,14 +48,22 @@
     own_table = jnp.where(j == rank_col, own_label, 0).astype(F32).astype(BF16)
     halo_table = jnp.where(j == halo_slot_col, halo_label, 0).astype(F32).astype(BF16)
 
-    q = iota((8 * n, n), 0)
-    pick = ones_where((q == target * 8 + rank_row) | (q == halo_target * 8 + halo_slot))
-    pick_own = ones_where(q == target * 8 + 6)
-    pick_halo = ones_where(q == halo_target * 8 + 6)
-    out = jnp.dot(pick, lat_ref[...], preferred_element_type=F32)
-    out += jnp.dot(pick_own, own_table, preferred_element_type=F32)
-    out += jnp.dot(pick_halo, halo_table, preferred_element_type=F32)
-    out_ref[...] = out.astype(BF16)
+    fetch.wait()
+    outs = []
+    for chunk in range(4):
+        rows = pl.ds(2 * n * chunk, 2 * n)
+        q = iota((2 * n, n), 0) + 2 * n * chunk
+        pick = ones_where((q == target * 8 + rank_row) | (q == halo_target * 8 + halo_slot))
+        pick_own = ones_where(q == target * 8 + 6)
+        pick_halo = ones_where(q == halo_target * 8 + 6)
+        out = jnp.dot(pick, lat_ref[...], preferred_element_type=F32)
+        out += jnp.dot(pick_own, own_table, preferred_element_type=F32)
+        out += jnp.dot(pick_halo, halo_table, preferred_element_type=F32)
+        out_ref[rows, :] = out.astype(BF16)
+        outs.append(pltpu.make_async_copy(out_ref.at[rows], out_hbm.at[rows], out_sems.at[chunk]))
+        outs[-1].start()
+    for copy in outs:
+        copy.wait()
 
 
 def route_kernel(inbox_ref, after_ref, out_ref):
@@ -364,11 +374,17 @@
 def local(latents, grid_slot, w_in, b_in, gain_in, w_up, b_up, gain_res, w_res, b_res):
     outbox = pl.pallas_call(
         outbox_kernel,
-        out_shape=jax.ShapeDtypeStruct((1024, 128), BF16),
-        in_specs=[VMEM_SPEC] * 2,
-        out_specs=VMEM_SPEC,
+        out_shape=pltpu.HBM((1024, 128), BF16),
+        in_specs=[VMEM_SPEC, HBM_SPEC],
+        out_specs=HBM_SPEC,
+        scratch_shapes=[
+            pltpu.VMEM((128, 128), BF16),
+            pltpu.VMEM((1024, 128), BF16),
+            pltpu.SemaphoreType.DMA,
+            pltpu.SemaphoreType.DMA((4,)),
+        ],
         name="outbox",
-    )(grid_slot.reshape(1, 128), latents)
+    )(grid_slot.reshape(1, 128), pltpu.with_memory_space_constraint(latents, pltpu.HBM))
     inbox = lax.all_to_all(
         outbox.reshape(128, 8, 128), ("seq", "tile"), split_axis=0, concat_axis=0, tiled=True
     )

time: 50.7 us -> 51.2 us (level)
  no operation moved by 1% of the time
where the time goes in v8:
time: 51.2 us; the launch traced here: 50.9 us
  Pallas kernels  24.7 us (48%)
  starting transfers between devices  11.5 us (22%)
  blocking collectives  7.84 us (15%)
  waiting for transfers between devices  6.73 us (13%)
    pallas_call x1, Pallas kernels, decode(): pl.pallas_call(decode_kernel, out_shape=jax.ShapeDtypeStruct((16, 8, 6144...  16.8 us
    all_to_all x1, starting transfers between devices, local(): lax.all_to_all(outbox.reshape(128, 8, 128), ('seq', 'tile'), split_axis=0...  11.5 us
    all_to_all x1, blocking collectives, local(): lax.all_to_all(routed.reshape(8, 48, 128), 'seq', split_axis=0, concat_ax...  7.84 us
    all_to_all x1, waiting for transfers between devices, local(): lax.all_to_all(outbox.reshape(128, 8, 128), ('seq', 'tile'), split_axis=0...  6.73 us
    pallas_call x1, Pallas kernels, local(): pl.pallas_call(prepare_kernel, out_shape=[jax.ShapeDtypeStruct((768, 384)...  4.73 us
    pallas_call x1, Pallas kernels, local(): pl.pallas_call(outbox_kernel, out_shape=pltpu.HBM((1024, 128), BF16), in_...  2.5 us
  transfers between devices with their start and end apart: 1, of which 1 were waited for; matrix products, arithmetic and copies ran while one was open for 0% of the time, Pallas kernels for 9%

profile of v8, /device:TPU:1, one launch (start us, length us, event | category | flops | bytes accessed | tf_op | source)
XLA Modules:
  0.0 50.9 jit_solution(13942419741324961224)
XLA Ops:
  0.0 2.5 %outbox.1 = bf16[1024,128]{1,0:T(8,128)(2,1)} custom-call(s32[1,128]{1,0:T(1,128)} %bitcast.13, bf16[128,128]{1,0:T(8,128)(2,1)} %lat_hbm.1), custom_call_target="tpu_custom_call" | custom-call | tf_op jit(solution)/shard_map/outbox/pallas_call | solution.py:375
  2.5 11.5 %all-to-all-start = ((bf16[128,8,128]{2,1,0:T(8,128)(2,1)}), bf16[128,8,128]{2,1,0:T(8,128)(2,1)S(1)}, u32[]{:S(2)}, u32[]{:S(2)}) async-start(bf16[128,8,128]{2,1,0:T(8,128)(2,1)} %bitcast.12), calls=%async_computation | async-start | bytes 524288 | tf_op jit(solution)/shard_map/all_to_all | solution.py:388
  14.0 4.7 %prepare.1 = (bf16[768,384]{1,0:T(8,128)(2,1)S(1)}, bf16[768,1536]{1,0:T(8,128)(2,1)}, bf16[192,7168]{1,0:T(8,128)(2,1)}, bf16[192,7168]{1,0:T(8,128)(2,1)}, f32[8,384]{1,0:T(8,128)S(1)}) custom-call(bf16[432,384]{1,0:T(8,128)(2,1)} %win_hbm.1, bf16[192,3456]{1,0:T(8,128)(2,1)} %bitcast.11, bf16[192,5184]{1,0:T(8,128)(2,1)} %bitcast.10, f32[384]{0:T(512)} %bin_hbm.1, ...), custom_call_target="tpu_custom_call" | custom-call | flops 10000000 | bytes 16000000 | tf_op jit(solution)/shard_map/prepare/pallas_call | solution.py:391
  18.8 6.7 %all-to-all-done = bf16[128,8,128]{2,1,0:T(8,128)(2,1)S(1)} async-done(((bf16[128,8,128]{2,1,0:T(8,128)(2,1)}), bf16[128,8,128]{2,1,0:T(8,128)(2,1)S(1)}, u32[]{:S(2)}, u32[]{:S(2)}) %all-to-all-start) | async-done | bytes 262176 | tf_op jit(solution)/shard_map/all_to_all | solution.py:388
  25.5 0.6 %route.1 = bf16[384,128]{1,0:T(8,128)(2,1)S(1)} custom-call(bf16[1024,128]{1,0:T(8,128)(2,1)S(1)} %bitcast.7, f32[8,384]{1,0:T(8,128)S(1)} %get-tuple-element.10.after_ref.vec_ref), custom_call_target="tpu_custom_call" | custom-call | tf_op jit(solution)/shard_map/route/pallas_call | solution.py:427
  26.1 7.8 %all_to_all.10 = bf16[8,48,128]{2,1,0:T(8,128)(2,1)S(1)} all-to-all(bf16[8,48,128]{2,1,0:T(8,128)(2,1)S(1)} %bitcast.9), channel_id=1, replica_groups=mesh['seq'=8,'tile'=16] {'seq'}, dimensions={0} | all-to-all | bytes 196608 | tf_op jit(solution)/shard_map/all_to_all | solution.py:435
  34.0 16.8 %decode.1 = bf16[16,8,6144]{2,1,0:T(8,128)(2,1)} custom-call(bf16[384,128]{1,0:T(8,128)(2,1)S(1)} %bitcast.8, bf16[768,384]{1,0:T(8,128)(2,1)S(1)} %get-tuple-element.11.w1_ref, bf16[768,1536]{1,0:T(8,128)(2,1)} %get-tuple-element.12.wc_hbm, bf16[192,7168]{1,0:T(8,128)(2,1)} %get-tuple-element.13.w0_hbm, bf16[192,7168]{1,0:T(8,128)(2,1)} %get-tuple-element.14.wp_hbm, ...), custom_call_target="tpu_custom_call" | custom-call | tf_op jit(solution)/shard_map/decode/pallas_call | solution.py:442
Async XLA Ops:
  2.5 23.0 %all-to-all-start = ((bf16[128,8,128]{2,1,0:T(8,128)(2,1)}), bf16[128,8,128]{2,1,0:T(8,128)(2,1)S(1)}, u32[]{:S(2)}, u32[]{:S(2)}) async-start(bf16[128,8,128]{2,1,0:T(8,128)(2,1)} %bitcast.12), calls=%async_computation | async-start | bytes 524288 | tf_op jit(solution)/shard_map/all_to_all | solution.py:388
